TPU v7x, 512 devices: a whole 4x8x8 slice. The times are simulated.
512 devices in a mesh: rep: 4 (over z_lo), fsdp: 16 (over y, core), tp: 8 (over z_hi, x).
Axes of the slice: x: 4, y: 8, z: 8 (z_hi: 2, z_lo: 4; z = z_hi * 4 + z_lo), core: 2. Of those that a mesh axis runs over, the one named last changes fastest.
Arguments:
- delta_attn: float32 [4, 4, 768, 768], P('rep', None, 'fsdp', 'tp'), may hold values from -4 to 4
- delta_in: float32 [4, 768, 3072], P('rep', 'fsdp', 'tp'), may hold values from -4 to 4
- delta_out: float32 [4, 3072, 768], P('rep', 'fsdp', 'tp'), may hold values from -4 to 4
- delta_small: float32 [4, 1920], P('rep'), may hold values from -4 to 4
- emb_left: float32 [4, 8, 4016, 64], P('rep', 'tp', 'fsdp'), may hold values from -6 to 6
- emb_right: float32 [4, 64, 768], P('rep'), may hold values from -0.75 to 0.75
- anchor_attn: float32 [8, 294912], P('tp', 'fsdp'), may hold values from -6 to 6
- anchor_in: float32 [8, 294912], P('tp', 'fsdp'), may hold values from -6 to 6
- anchor_out: float32 [8, 294912], P('tp', 'fsdp'), may hold values from -6 to 6
- anchor_small: float32 [1920], P('fsdp'), may hold values from -6 to 6
- anchor_emb: float32 [8, 16, 4, 48192], P('tp', 'fsdp', 'rep'), may hold values from -6 to 6
- moment_attn: float32 [8, 294912], P('tp', 'fsdp'), may hold values from -4 to 4
- moment_in: float32 [8, 294912], P('tp', 'fsdp'), may hold values from -4 to 4
- moment_out: float32 [8, 294912], P('tp', 'fsdp'), may hold values from -4 to 4
- moment_small: float32 [1920], P('fsdp'), may hold values from -4 to 4
- moment_emb: float32 [8, 16, 4, 48192], P('tp', 'fsdp', 'rep'), may hold values from -4 to 4
Outputs:
- new_attn: float32 [4, 768, 768], P(None, 'fsdp', 'tp')
- new_in: float32 [768, 3072], P('fsdp', 'tp')
- new_out: float32 [3072, 768], P('fsdp', 'tp')
- new_small: float32 [1920], replicated
- new_emb: float32 [32128, 768], P('tp', 'fsdp')
- next_attn: float32 [8, 294912], P('tp', 'fsdp')
- next_in: float32 [8, 294912], P('tp', 'fsdp')
- next_out: float32 [8, 294912], P('tp', 'fsdp')
- next_small: float32 [1920], P('fsdp')
- next_emb: float32 [8, 16, 4, 48192], P('tp', 'fsdp', 'rep')
All inputs are finite; a program needn't handle non-finite values.
Results may differ from a plain program's by a relative error of at most 0.000071.
Values sent between devices are 32-bit elements; how exact they have to be, the bound alone decides.
A program may use at most 64 MiB of HBM per device.

v0:
```python
import jax
import jax.numpy as jnp
from jax import lax
from jax.sharding import PartitionSpec as P

OUTER_RATE = 0.7
MOMENTUM_COEF = 0.9


def nesterov(anchor, moment, mean_delta):
    moment_next = MOMENTUM_COEF * moment + mean_delta
    updated = anchor - OUTER_RATE * (mean_delta + MOMENTUM_COEF * moment_next)
    return (updated, moment_next)


def to_blocks(matrix, lead, shards):
    local_rows = matrix.shape[-2]
    width = matrix.shape[-1] // shards
    shaped = matrix.reshape(lead, local_rows, shards, width)
    return jnp.transpose(shaped, (2, 3, 0, 1))


def from_blocks(blocks):
    shards, width, lead, local_rows = blocks.shape
    return jnp.transpose(blocks, (2, 3, 0, 1)).reshape(lead, local_rows, shards * width)


def on_device(
    delta_attn,
    delta_in,
    delta_out,
    delta_small,
    emb_left,
    emb_right,
    anchor_attn,
    anchor_in,
    anchor_out,
    anchor_small,
    anchor_emb,
    moment_attn,
    moment_in,
    moment_out,
    moment_small,
    moment_emb,
):
    groups = lax.axis_size("rep")
    shards = lax.axis_size("fsdp")
    send_attn = to_blocks(delta_attn[0], 4, shards)
    send_in = to_blocks(delta_in[0][None], 1, shards)
    send_out = to_blocks(delta_out[0][None], 1, shards)
    flat_attn, flat_in, flat_out = (
        lax.all_to_all(send_attn, "fsdp", split_axis=0, concat_axis=3, tiled=True),
        lax.all_to_all(send_in, "fsdp", split_axis=0, concat_axis=3, tiled=True),
        lax.all_to_all(send_out, "fsdp", split_axis=0, concat_axis=3, tiled=True),
    )
    block_shapes = (flat_attn.shape, flat_in.shape, flat_out.shape)
    portion = anchor_small.shape[0]
    small_local = lax.dynamic_slice_in_dim(
        delta_small[0], lax.axis_index("fsdp") * portion, portion, 0
    )[None, :]
    differences = (
        flat_attn.reshape(flat_attn.shape[1] * flat_attn.shape[2], flat_attn.shape[3]),
        flat_in.reshape(flat_in.shape[1], flat_in.shape[3]),
        flat_out.reshape(flat_out.shape[1], flat_out.shape[3]),
        small_local,
    )
    anchors = (
        anchor_attn.reshape(differences[0].shape),
        anchor_in.reshape(differences[1].shape),
        anchor_out.reshape(differences[2].shape),
        anchor_small[None, :],
    )
    moments = (
        moment_attn.reshape(differences[0].shape),
        moment_in.reshape(differences[1].shape),
        moment_out.reshape(differences[2].shape),
        moment_small[None, :],
    )
    totals = lax.psum((differences[0], differences[1], differences[2], differences[3]), "rep")
    updated_list = []
    moment_list = []
    for summed, anchor_part, moment_part in zip(totals, anchors, moments):
        updated, moment_next = nesterov(anchor_part, moment_part, summed / groups)
        updated_list.append(updated)
        moment_list.append(moment_next)
    back_attn = updated_list[0].reshape(block_shapes[0])
    back_in = updated_list[1].reshape(block_shapes[1])
    back_out = updated_list[2].reshape(block_shapes[2])
    train_attn, train_in, train_out = (
        lax.all_to_all(back_attn, "fsdp", split_axis=3, concat_axis=0, tiled=True),
        lax.all_to_all(back_in, "fsdp", split_axis=3, concat_axis=0, tiled=True),
        lax.all_to_all(back_out, "fsdp", split_axis=3, concat_axis=0, tiled=True),
    )
    new_attn = from_blocks(train_attn)
    new_in = from_blocks(train_in)[0]
    new_out = from_blocks(train_out)[0]
    new_small = lax.all_gather(updated_list[3].reshape(portion), "fsdp", axis=0, tiled=True)
    left_local = emb_left[0, 0]
    right_local = emb_right[0]
    block_rows = left_local.shape[0]
    column_count = right_local.shape[1] // groups
    product_term = jnp.dot(
        left_local, right_local, precision=lax.Precision.HIGHEST, preferred_element_type=jnp.float32
    )
    summed_emb = lax.psum_scatter(product_term, "rep", scatter_dimension=1, tiled=True)
    anchor_rows = anchor_emb[0, 0, 0].reshape(block_rows, column_count)
    moment_rows = moment_emb[0, 0, 0].reshape(block_rows, column_count)
    new_emb_part, next_emb_part = nesterov(anchor_rows, moment_rows, summed_emb / groups)
    full_rows = lax.all_gather(new_emb_part, "rep", axis=1, tiled=True)
    new_emb = lax.all_to_all(full_rows, "fsdp", split_axis=1, concat_axis=0, tiled=True)
    return (
        new_attn,
        new_in,
        new_out,
        new_small,
        new_emb,
        moment_list[0].reshape(moment_attn.shape),
        moment_list[1].reshape(moment_in.shape),
        moment_list[2].reshape(moment_out.shape),
        moment_list[3].reshape(moment_small.shape),
        next_emb_part.reshape(moment_emb.shape),
    )


def solution(mesh):
    placed = (
        P("rep", None, "fsdp", "tp"),
        P("rep", "fsdp", "tp"),
        P("rep", "fsdp", "tp"),
        P("rep", None),
        P("rep", "tp", "fsdp", None),
        P("rep", None, None),
        P("tp", "fsdp"),
        P("tp", "fsdp"),
        P("tp", "fsdp"),
        P("fsdp"),
        P("tp", "fsdp", "rep", None),
        P("tp", "fsdp"),
        P("tp", "fsdp"),
        P("tp", "fsdp"),
        P("fsdp"),
        P("tp", "fsdp", "rep", None),
    )
    return jax.shard_map(
        on_device,
        mesh=mesh,
        in_specs=placed,
        out_specs=(
            P(None, "fsdp", "tp"),
            P("fsdp", "tp"),
            P("fsdp", "tp"),
            P(),
            P("tp", "fsdp"),
            P("tp", "fsdp"),
            P("tp", "fsdp"),
            P("tp", "fsdp"),
            P("fsdp"),
            P("tp", "fsdp", "rep", None),
        ),
        check_vma=False,
    )
```

profile of v0, /device:TPU:57, one launch (start us, length us, event | category | flops | bytes accessed | tf_op | source)
XLA Modules:
  0.0 242.4 jit_solution(11660199578842059813)
XLA Ops:
  7.2 1.1 copy.88
  8.2 0.8 reshape.155
  9.1 8.8 %all-to-all-start.2 = ((f32[16,1,1152]{2,1,0:T(1,128)}), f32[16,1,1152]{2,1,0:T(1,128)S(1)}, u32[]{:S(2)}, u32[]{:S(2)}) async-start(f32[16,1,1152]{2,1,0:T(1,128)} %reshape.155), calls=%async_computation.2 | async-start | bytes 147456 | tf_op jit(solution)/shard_map/all_to_all | solution.py:53
  17.9 1.0 copy.83
  18.9 0.9 reshape.151
  19.8 3.7 %all-to-all-done.2 = f32[16,1,1152]{2,1,0:T(1,128)S(1)} async-done(((f32[16,1,1152]{2,1,0:T(1,128)}), f32[16,1,1152]{2,1,0:T(1,128)S(1)}, u32[]{:S(2)}, u32[]{:S(2)}) %all-to-all-start.2) | async-done | bytes 73760 | tf_op jit(solution)/shard_map/all_to_all | solution.py:53
  23.5 5.9 %all-to-all-start = ((f32[16,1,1152]{2,1,0:T(1,128)}), f32[16,1,1152]{2,1,0:T(1,128)S(1)}, u32[]{:S(2)}, u32[]{:S(2)}) async-start(f32[16,1,1152]{2,1,0:T(1,128)} %reshape.151), calls=%async_computation | async-start | bytes 147456 | tf_op jit(solution)/shard_map/all_to_all | solution.py:52
  29.3 1.6 copy.94
  31.5 0.8 reduce.28
  32.5 2.4 all-to-all-done
  34.9 5.9 %all-to-all-start.4 = ((f32[16,6,1,192]{3,2,1,0:T(1,128)}), f32[16,6,1,192]{3,2,1,0:T(1,128)S(1)}, u32[]{:S(2)}, u32[]{:S(2)}) async-start(f32[16,6,1,192]{3,2,1,0:T(1,128)} %bitcast.21), calls=%async_computation.4 | async-start | bytes 196608 | tf_op jit(solution)/shard_map/all_to_all | solution.py:54
  40.9 0.8 reshape.93
  41.7 0.8 reduce.27
  42.8 0.8 reshape.89
  43.5 3.1 %all-to-all-done.4 = f32[16,6,1,192]{3,2,1,0:T(1,128)S(1)} async-done(((f32[16,6,1,192]{3,2,1,0:T(1,128)}), f32[16,6,1,192]{3,2,1,0:T(1,128)S(1)}, u32[]{:S(2)}, u32[]{:S(2)}) %all-to-all-start.4) | async-done | bytes 73760 | tf_op jit(solution)/shard_map/all_to_all | solution.py:54
  47.7 1.7 fusion
  49.9 0.8 reduce.26
  51.3 0.8 reduce.25
  53.4 0.8 reduce.24
  57.1 0.8 copy.99
  57.9 43.8 %all-reduce.4.cloned.1.call-done = (f32[24,768]{1,0:T(8,128)}, f32[24,768]{1,0:T(8,128)}, f32[6,3072]{1,0:T(8,128)}) async-done(((f32[24,768]{1,0:T(8,128)}, f32[24,768]{1,0:T(8,128)}, f32[6,3072]{1,0:T(8,128)}), (f32[24,768]{1,0:T(8,128)}, f32[24,768]{1,0:T(8,128)}, f32[6,3072]{1,0:T(8,128)})) %all-reduce.4.cloned.1.call-update) | async-done | bytes 221200 | tf_op jit(solution)/shard_map/psum | solution.py:79
  101.7 1.6 fusion.2
  103.2 1.6 copy.96
  104.8 13.7 %reduce.32 = f32[3072,6]{1,0:T(8,128)S(1)} reduce(f32[3072,1,1,6]{3,2,1,0:T(1,128)S(1)} %bitcast.106, f32[]{:T(128)} %broadcast.90), dimensions={1,2}, to_apply=%bitcast.99.reduce_sub_computation | reduce | bytes 147460
  118.6 1.9 reshape.159
  120.5 9.7 %all-to-all-start.5 = ((f32[16,1,1152]{2,1,0:T(1,128)}), f32[16,1,1152]{2,1,0:T(1,128)S(1)}, u32[]{:S(2)}, u32[]{:S(2)}) async-start(f32[16,1,1152]{2,1,0:T(1,128)} %reshape.159), calls=%async_computation.5 | async-start | bytes 147456 | tf_op jit(solution)/shard_map/all_to_all | solution.py:92
  131.1 1.6 reduce.30
  132.7 0.9 reshape.157
  135.1 2.5 %reshape.153 = f32[16,1,1152]{2,1,0:T(1,128)} reshape(f32[768,1,4,6]{3,2,1,0:T(4,128)S(1)} %bitcast.103) | data formatting | bytes 147456
  137.6 7.2 %all-to-all-start.3 = ((f32[16,1,1152]{2,1,0:T(1,128)}), f32[16,1,1152]{2,1,0:T(1,128)S(1)}, u32[]{:S(2)}, u32[]{:S(2)}) async-start(f32[16,1,1152]{2,1,0:T(1,128)} %reshape.157), calls=%async_computation.3 | async-start | bytes 147456 | tf_op jit(solution)/shard_map/all_to_all | solution.py:91
  144.8 1.0 multiply_add_fusion
  145.9 4.4 %all-to-all-done.3 = f32[16,1,1152]{2,1,0:T(1,128)S(1)} async-done(((f32[16,1,1152]{2,1,0:T(1,128)}), f32[16,1,1152]{2,1,0:T(1,128)S(1)}, u32[]{:S(2)}, u32[]{:S(2)}) %all-to-all-start.3) | async-done | bytes 73760 | tf_op jit(solution)/shard_map/all_to_all | solution.py:91
  150.3 6.0 %all-to-all-start.1 = ((f32[16,1,1152]{2,1,0:T(1,128)}), f32[16,1,1152]{2,1,0:T(1,128)S(1)}, u32[]{:S(2)}, u32[]{:S(2)}) async-start(f32[16,1,1152]{2,1,0:T(1,128)} %reshape.153), calls=%async_computation.1 | async-start | bytes 147456 | tf_op jit(solution)/shard_map/all_to_all | solution.py:90
  156.3 16.1 %all_gather.7 = f32[251,768]{0,1:T(8,128)} all-gather(f32[251,192]{0,1:T(8,128)S(1)} %get-tuple-element.54), channel_id=1, replica_groups=mesh['rep'=4,'fsdp'=16,'tp'=8] {'rep'}, dimensions={1}, use_global_device_ids=true | all-gather | bytes 963840 | tf_op jit(solution)/shard_map/all_gather | solution.py:109
  172.4 9.4 %all-to-all-start.6 = ((f32[251,16,48]{0,2,1:T(8,128)}), f32[251,16,48]{0,2,1:T(8,128)S(1)}, u32[]{:S(2)}, u32[]{:S(2)}) async-start(f32[251,16,48]{0,2,1:T(8,128)} %bitcast.35), calls=%async_computation.7 | async-start | bytes 1572864 | tf_op jit(solution)/shard_map/all_to_all | solution.py:110
  181.8 1.3 dynamic-slice.1
  184.4 8.8 %psum.31 = f32[1,120]{1,0:T(1,128)S(1)} all-reduce(f32[1,120]{1,0:T(1,128)S(1)} %constant_dynamic-slice_fusion), channel_id=1, replica_groups=mesh['rep'=4,'fsdp'=16,'tp'=8] {'rep'}, use_global_device_ids=true, to_apply=%region_3.0 | all-reduce | flops 120 | bytes 960 | tf_op jit(solution)/shard_map/psum | solution.py:79
  193.3 24.9 %all-reduce = f32[1920]{0:T(1024)} all-reduce(f32[1920]{0:T(1024)S(1)} %bitcast_dynamic-update-slice_fusion), channel_id=2, replica_groups=mesh['rep'=4,'fsdp'=16,'tp'=8] {'fsdp'}, use_global_device_ids=true, to_apply=%add | all-reduce | flops 1920 | bytes 15360 | tf_op jit(solution)/shard_map/all_gather | solution.py:97
  220.9 0.8 reduce.33
  221.7 2.5 %reshape.160 = f32[3072,1,1,6]{3,2,1,0:T(1,128)S(1)} reshape(f32[16,1152]{1,0:T(8,128)S(1)} %reduce.33) | data formatting | bytes 147456
  225.7 0.8 reduce.31
  227.5 0.7 copy.104
  228.2 0.8 reduce.29
  229.0 2.0 reshape.154
  231.1 0.8 copy.106
  231.9 0.8 copy.103
  232.8 0.9 reshape.103
  234.2 1.3 all_to_all.110
  (100 shorter events, 16.2 us)
Async XLA Ops:
  7.2 40.5 %copy-start = (f32[1,64,768]{2,1,0:T(8,128)S(1)}, f32[1,64,768]{2,1,0:T(8,128)}, u32[]{:S(2)}) copy-start(f32[1,64,768]{2,1,0:T(8,128)} %param.21) | copy-start | bytes 589828
  9.1 14.4 %all-to-all-start.2 = ((f32[16,1,1152]{2,1,0:T(1,128)}), f32[16,1,1152]{2,1,0:T(1,128)S(1)}, u32[]{:S(2)}, u32[]{:S(2)}) async-start(f32[16,1,1152]{2,1,0:T(1,128)} %reshape.155), calls=%async_computation.2 | async-start | bytes 147456 | tf_op jit(solution)/shard_map/all_to_all | solution.py:53
  23.5 11.4 %all-to-all-start = ((f32[16,1,1152]{2,1,0:T(1,128)}), f32[16,1,1152]{2,1,0:T(1,128)S(1)}, u32[]{:S(2)}, u32[]{:S(2)}) async-start(f32[16,1,1152]{2,1,0:T(1,128)} %reshape.151), calls=%async_computation | async-start | bytes 147456 | tf_op jit(solution)/shard_map/all_to_all | solution.py:52
  32.4 15.3 %copy-start.21 = (f32[1,1,251,64]{2,3,1,0:T(8,128)S(1)}, f32[1,1,251,64]{2,3,1,0:T(8,128)}, u32[]{:S(2)}) copy-start(f32[1,1,251,64]{2,3,1,0:T(8,128)} %param.20) | copy-start | bytes 192772
  34.9 11.7 %all-to-all-start.4 = ((f32[16,6,1,192]{3,2,1,0:T(1,128)}), f32[16,6,1,192]{3,2,1,0:T(1,128)S(1)}, u32[]{:S(2)}, u32[]{:S(2)}) async-start(f32[16,6,1,192]{3,2,1,0:T(1,128)} %bitcast.21), calls=%async_computation.4 | async-start | bytes 196608 | tf_op jit(solution)/shard_map/all_to_all | solution.py:54
  40.8 60.9 %all-reduce.4.cloned.1.call-start = ((), (), s32[]{:S(2)}) async-start(), calls=%async_computation.9 | async-start | bytes 491520 | tf_op jit(solution)/shard_map/psum | solution.py:79
  42.7 7.2 %copy-start.13 = (f32[1,18432]{1,0:T(1,128)S(1)}, f32[1,18432]{1,0:T(1,128)}, u32[]{:S(2)}) copy-start(f32[1,18432]{1,0:T(1,128)} %param.24) | copy-start | bytes 221188
  42.7 8.0 %copy-start.17 = (f32[1,18432]{1,0:T(1,128)S(1)}, f32[1,18432]{1,0:T(1,128)}, u32[]{:S(2)}) copy-start(f32[1,18432]{1,0:T(1,128)} %param.29) | copy-start | bytes 221188
  42.7 8.0 %copy-start.18 = (f32[1,18432]{1,0:T(1,128)S(1)}, f32[1,18432]{1,0:T(1,128)}, u32[]{:S(2)}) copy-start(f32[1,18432]{1,0:T(1,128)} %param.28) | copy-start | bytes 221188
  46.6 4.7 %copy-start.14 = (f32[1,18432]{1,0:T(1,128)S(1)}, f32[1,18432]{1,0:T(1,128)}, u32[]{:S(2)}) copy-start(f32[1,18432]{1,0:T(1,128)} %param.23) | copy-start | bytes 221188
  47.4 6.0 %copy-start.15 = (f32[1,18432]{1,0:T(1,128)S(1)}, f32[1,18432]{1,0:T(1,128)}, u32[]{:S(2)}) copy-start(f32[1,18432]{1,0:T(1,128)} %param.22) | copy-start | bytes 221188
  47.4 7.5 %copy-start.16 = (f32[1,18432]{1,0:T(1,128)S(1)}, f32[1,18432]{1,0:T(1,128)}, u32[]{:S(2)}) copy-start(f32[1,18432]{1,0:T(1,128)} %param.27) | copy-start | bytes 221188
  47.4 8.3 %copy-start.11 = (f32[1,1,1,48192]{3,2,1,0:T(1,128)S(1)}, f32[1,1,1,48192]{3,2,1,0:T(1,128)}, u32[]{:S(2)}) copy-start(f32[1,1,1,48192]{3,2,1,0:T(1,128)} %param.26) | copy-start | bytes 578308
  47.4 97.4 %reduce-scatter.2.cloned.1.call-start = ((), (), s32[]{:S(2)}) async-start(), calls=%async_computation.8 | async-start | bytes 983040 | tf_op jit(solution)/shard_map/reduce_scatter | solution.py:105
  49.4 7.0 %copy-start.12 = (f32[1,1,1,48192]{3,2,1,0:T(1,128)S(1)}, f32[1,1,1,48192]{3,2,1,0:T(1,128)}, u32[]{:S(2)}) copy-start(f32[1,1,1,48192]{3,2,1,0:T(1,128)} %param.31) | copy-start | bytes 578308
  118.5 11.6 %copy-start.9 = (f32[24,768]{1,0:T(8,128)S(1)}, f32[24,768]{1,0:T(8,128)}, u32[]{:S(2)}) copy-start(f32[24,768]{1,0:T(8,128)} %reshape.92) | copy-start | bytes 221188
  118.5 11.6 %copy-start.10 = (f32[24,768]{1,0:T(8,128)S(1)}, f32[24,768]{1,0:T(8,128)}, u32[]{:S(2)}) copy-start(f32[24,768]{1,0:T(8,128)} %mul.77) | copy-start | bytes 221188
  118.5 11.6 %copy-start.20 = (f32[24,768]{1,0:T(8,128)S(1)}, f32[24,768]{1,0:T(8,128)}, u32[]{:S(2)}) copy-start(f32[24,768]{1,0:T(8,128)} %get-tuple-element.51) | copy-start | bytes 221188
  118.6 15.1 %copy-start.7 = (f32[24,768]{1,0:T(8,128)S(1)}, f32[24,768]{1,0:T(8,128)}, u32[]{:S(2)}) copy-start(f32[24,768]{1,0:T(8,128)} %reshape.88) | copy-start | bytes 221188
  118.6 15.1 %copy-start.8 = (f32[24,768]{1,0:T(8,128)S(1)}, f32[24,768]{1,0:T(8,128)}, u32[]{:S(2)}) copy-start(f32[24,768]{1,0:T(8,128)} %mul.73) | copy-start | bytes 221188
  118.6 15.1 %copy-start.19 = (f32[24,768]{1,0:T(8,128)S(1)}, f32[24,768]{1,0:T(8,128)}, u32[]{:S(2)}) copy-start(f32[24,768]{1,0:T(8,128)} %get-tuple-element.50) | copy-start | bytes 221188
  120.5 17.1 %all-to-all-start.5 = ((f32[16,1,1152]{2,1,0:T(1,128)}), f32[16,1,1152]{2,1,0:T(1,128)S(1)}, u32[]{:S(2)}, u32[]{:S(2)}) async-start(f32[16,1,1152]{2,1,0:T(1,128)} %reshape.159), calls=%async_computation.5 | async-start | bytes 147456 | tf_op jit(solution)/shard_map/all_to_all | solution.py:92
  134.4 10.5 %copy-start.1 = (f32[251,192]{0,1:T(8,128)S(1)}, f32[251,192]{0,1:T(8,128)}, u32[]{:S(2)}) copy-start(f32[251,192]{0,1:T(8,128)} %copy.99) | copy-start | bytes 578308
  137.6 12.7 %all-to-all-start.3 = ((f32[16,1,1152]{2,1,0:T(1,128)}), f32[16,1,1152]{2,1,0:T(1,128)S(1)}, u32[]{:S(2)}, u32[]{:S(2)}) async-start(f32[16,1,1152]{2,1,0:T(1,128)} %reshape.157), calls=%async_computation.3 | async-start | bytes 147456 | tf_op jit(solution)/shard_map/all_to_all | solution.py:91
  145.8 47.4 %copy-start.22 = (f32[120]{0:T(128)S(1)}, f32[120]{0:T(128)}, u32[]{:S(2)}) copy-start(f32[120]{0:T(128)} %param.25) | copy-start | bytes 1444
  145.8 47.4 %copy-start.23 = (f32[120]{0:T(128)S(1)}, f32[120]{0:T(128)}, u32[]{:S(2)}) copy-start(f32[120]{0:T(128)} %param.30) | copy-start | bytes 1444
  145.8 72.9 %copy-start.2 = (f32[1,1,6,3072]{3,2,1,0:T(8,128)S(1)}, f32[1,1,6,3072]{3,2,1,0:T(8,128)}, u32[]{:S(2)}) copy-start(f32[1,1,6,3072]{3,2,1,0:T(8,128)} %get-tuple-element.55) | copy-start | bytes 221188
  145.9 73.6 %copy-start.5 = (f32[1,1,24,768]{3,2,1,0:T(8,128)S(1)}, f32[1,1,24,768]{3,2,1,0:T(8,128)}, u32[]{:S(2)}) copy-start(f32[1,1,24,768]{3,2,1,0:T(8,128)} %get-tuple-element.57) | copy-start | bytes 221188
  145.9 74.3 %copy-start.6 = (f32[1,1,24,768]{3,2,1,0:T(8,128)S(1)}, f32[1,1,24,768]{3,2,1,0:T(8,128)}, u32[]{:S(2)}) copy-start(f32[1,1,24,768]{3,2,1,0:T(8,128)} %get-tuple-element.59) | copy-start | bytes 221188
  150.3 70.6 %copy-start.3 = (f32[16,1,1152]{2,1,0:T(1,128)}, f32[16,1,1152]{2,1,0:T(1,128)S(1)}, u32[]{:S(2)}) copy-start(f32[16,1,1152]{2,1,0:T(1,128)S(1)} %all-to-all-done.3) | copy-start | bytes 221188
  150.3 22.1 %all-to-all-start.1 = ((f32[16,1,1152]{2,1,0:T(1,128)}), f32[16,1,1152]{2,1,0:T(1,128)S(1)}, u32[]{:S(2)}, u32[]{:S(2)}) async-start(f32[16,1,1152]{2,1,0:T(1,128)} %reshape.153), calls=%async_computation.1 | async-start | bytes 147456 | tf_op jit(solution)/shard_map/all_to_all | solution.py:90
  172.4 61.3 %all-to-all-start.6 = ((f32[251,16,48]{0,2,1:T(8,128)}), f32[251,16,48]{0,2,1:T(8,128)S(1)}, u32[]{:S(2)}, u32[]{:S(2)}) async-start(f32[251,16,48]{0,2,1:T(8,128)} %bitcast.35), calls=%async_computation.7 | async-start | bytes 1572864 | tf_op jit(solution)/shard_map/all_to_all | solution.py:110
  224.2 1.5 copy-start.4
Sparse Core Ops, SparseCore 0:
  47.5 54.1 all-reduce.3
  105.3 31.0 reduce-scatter.1
where the time goes:
time: 247 us; the launch traced here: 242 us
  waiting for transfers between devices  57.4 us (23%)
  starting transfers between devices  53.1 us (21%)
  blocking collectives  49.8 us (20%)
  local copies, waits for them, and re-layouts  37.2 us (15%)
  other arithmetic  27.9 us (11%)
  between operations  15.3 us (6%)
    psum x1, waiting for transfers between devices, on_device(): lax.psum((differences[0], differences[1], differences[2], differences[3])...  43.8 us
    all_gather x1, blocking collectives, on_device(): lax.all_gather(updated_list[3].reshape(portion), 'fsdp', axis=0, tiled=True)  24.9 us
    unnamed x70, local copies, waits for them, and re-layouts  22.5 us
    unnamed x10, other arithmetic  21.2 us
    all_gather x1, blocking collectives, on_device(): full_rows = lax.all_gather(new_emb_part, 'rep', axis=1, tiled=True)  16.1 us
    all_to_all x1, starting transfers between devices, on_device(): lax.all_to_all(back_out, 'fsdp', split_axis=3, concat_axis=0, tiled=True)  9.67 us
    all_to_all x1, starting transfers between devices, on_device(): lax.all_to_all(full_rows, 'fsdp', split_axis=1, concat_axis=0, tiled=True)  9.35 us
    all_to_all x1, starting transfers between devices, on_device(): lax.all_to_all(send_in, 'fsdp', split_axis=0, concat_axis=3, tiled=True)  8.84 us
  transfers between devices with their start and end apart: 9, of which 5 were waited for; matrix products, arithmetic and copies ran while one was open for 26% of the time, Pallas kernels for 0%

commit v1 on v0

v1 whole, which is shorter than its diff:
```python
import jax
import jax.numpy as jnp
from jax import lax
from jax.experimental import pallas as pl
from jax.experimental.pallas import tpu as pltpu
from jax.sharding import PartitionSpec as P

OUTER_RATE = 0.7
MOMENTUM_COEF = 0.9
G = 4
F = 16
ROWS = 251
KEEP = OUTER_RATE * MOMENTUM_COEF * MOMENTUM_COEF
STEP = OUTER_RATE * (1.0 + MOMENTUM_COEF) / G
MEAN = 1.0 / G


def dot(a, b, ca, cb):
    return lax.dot_general(
        a, b, (((ca,), (cb,)), ((), ())), precision=lax.Precision.HIGHEST, preferred_element_type=jnp.float32
    )


def sixth(d):
    return (d * 43) >> 8


def spread_rows():
    row = lax.broadcasted_iota(jnp.int32, (128, 96), 0)
    col = lax.broadcasted_iota(jnp.int32, (128, 96), 1)
    return (row == col + 2 * sixth(col)).astype(jnp.float32)


def pick_columns(q):
    row = lax.broadcasted_iota(jnp.int32, (384, 96), 0)
    col = lax.broadcasted_iota(jnp.int32, (384, 96), 1)
    return (row == col + 18 * sixth(col) + 6 * q).astype(jnp.float32)


def kernel(
    d_attn, d_in, d_out, d_small, left, right,
    a_attn, a_in, a_out, a_small, a_emb,
    m_attn, m_in, m_out, m_small, m_emb,
    new_attn, new_in, new_out, new_small, new_emb,
    next_attn, next_in, next_out, next_small, next_emb,
    lin, wide, widef, quart, quart_in, own_sum, sums, lpad, lt_own, lts, rts_own, rts, epad, et,
    amsg, arecv, umsg, urecv, gath,
    q_ss, q_rs, l_ss, l_rs, r_ss, r_rs, a_ss, a_rs, s_ss, s_rs, u_ss, u_rs, e_ss, up_ss, dn_ss, e_rs,
):
    f = lax.axis_index("fsdp")
    g = lax.axis_index("rep")

    def peer_f(d):
        return lax.rem(f + d, F)

    def peer_g(d):
        return lax.rem(g + d, G)

    bar = pltpu.get_barrier_semaphore()

    @pl.loop(1, F)
    def _(d):
        pl.semaphore_signal(bar, inc=1, device_id={"fsdp": peer_f(d)}, device_id_type=pl.DeviceIdType.MESH)

    @pl.loop(1, G)
    def _(d):
        pl.semaphore_signal(bar, inc=1, device_id={"rep": peer_g(d)}, device_id_type=pl.DeviceIdType.MESH)

    lpad[pl.ds(248, 8), :] = jnp.zeros((8, 64), jnp.float32)
    lpad[pl.ds(0, ROWS), :] = left[...]
    eye = (lax.broadcasted_iota(jnp.int32, (64, 64), 0) == lax.broadcasted_iota(jnp.int32, (64, 64), 1)).astype(jnp.float32)
    lt_own[...] = dot(eye, lpad[...], 1, 1)
    lts[g] = lt_own[...]
    for q in range(G):
        rts_own[q, :, 0:192] = right[:, q * 192 : (q + 1) * 192]
    rts[g] = rts_own[g]

    small = d_small[...]
    x_in = d_in[...]
    for q in range(G):
        quart[q, 0:48, 0:96] = d_attn[q * 48 : (q + 1) * 48, :]
        quart[q, 48:96, 0:96] = d_out[q * 48 : (q + 1) * 48, :]
        quart[q, 96:144, 0:96] = dot(x_in, pick_columns(q), 1, 0)
        quart[q, 144:160, 0:120] = small
    quart_in[g] = quart[g]

    pl.semaphore_wait(bar, F + G - 2)

    def left_copy(d):
        return pltpu.make_async_remote_copy(
            src_ref=lt_own, dst_ref=lts.at[g], send_sem=l_ss.at[d], recv_sem=l_rs.at[d],
            device_id={"rep": peer_g(d)}, device_id_type=pl.DeviceIdType.MESH)

    def right_copy(d):
        return pltpu.make_async_remote_copy(
            src_ref=rts_own.at[peer_g(d)], dst_ref=rts.at[g], send_sem=r_ss.at[d], recv_sem=r_rs.at[d],
            device_id={"rep": peer_g(d)}, device_id_type=pl.DeviceIdType.MESH)

    def quarter_copy(d):
        return pltpu.make_async_remote_copy(
            src_ref=quart.at[peer_g(d)], dst_ref=quart_in.at[g], send_sem=q_ss.at[d], recv_sem=q_rs.at[d],
            device_id={"rep": peer_g(d)}, device_id_type=pl.DeviceIdType.MESH)

    def sum_copy(d):
        return pltpu.make_async_remote_copy(
            src_ref=own_sum, dst_ref=sums.at[g], send_sem=s_ss.at[d], recv_sem=s_rs.at[d],
            device_id={"rep": peer_g(d)}, device_id_type=pl.DeviceIdType.MESH)

    def anchor_copy(d):
        return pltpu.make_async_remote_copy(
            src_ref=amsg.at[peer_f(d)], dst_ref=arecv.at[f], send_sem=a_ss.at[d], recv_sem=a_rs.at[d],
            device_id={"fsdp": peer_f(d)}, device_id_type=pl.DeviceIdType.MESH)

    def total_copy(d):
        return pltpu.make_async_remote_copy(
            src_ref=umsg.at[peer_f(d)], dst_ref=urecv.at[f], send_sem=u_ss.at[d], recv_sem=u_rs.at[d],
            device_id={"fsdp": peer_f(d)}, device_id_type=pl.DeviceIdType.MESH)

    def each(copy, n, what):
        @pl.loop(1, n)
        def _(d):
            getattr(copy(d), what)()

    each(left_copy, G, "start")
    each(right_copy, G, "start")
    each(quarter_copy, G, "start")

    amsg[...] = jnp.zeros((F, 8, 640), jnp.float32)
    lin[0] = a_attn[...] - KEEP * m_attn[...]
    lin[1] = a_out[...] - KEEP * m_out[...]
    lin[2] = a_in[...] - KEEP * m_in[...]
    for q in range(G):
        for s in range(6):
            wide[q, 0:6, s * 128 : (s + 1) * 128] = lin[0, pl.ds(q * 6 + s, 6, stride=24), :]
            wide[4 + q, 0:6, s * 128 : (s + 1) * 128] = lin[2, pl.ds(q * 36 + s, 6, stride=6), :]
    for s in range(24):
        widef[0:6, s * 128 : (s + 1) * 128] = lin[1, pl.ds(s, 6, stride=24), :]
    share = a_small[...] - KEEP * m_small[...]
    for t in range(F):
        for q in range(G):
            amsg[t, 0:6, q * 144 : q * 144 + 48] = wide[q, 0:6, t * 48 : (t + 1) * 48]
            amsg[t, 0:6, q * 144 + 48 : q * 144 + 96] = widef[0:6, t * 192 + q * 48 : t * 192 + q * 48 + 48]
            amsg[t, 0:6, q * 144 + 96 : q * 144 + 144] = wide[4 + q, 0:6, t * 48 : (t + 1) * 48]
        amsg[t, 6:7, 0:120] = share
    arecv[f] = amsg[f]
    each(anchor_copy, F, "start")

    each(left_copy, G, "wait_recv")
    each(right_copy, G, "wait_recv")
    u_emb = dot(lts[0], rts[0, :, 0:192], 0, 0)
    for k in range(1, G):
        u_emb = u_emb + dot(lts[k], rts[k, :, 0:192], 0, 0)
    u_emb = u_emb[0:ROWS, :]
    next_emb[...] = MOMENTUM_COEF * m_emb[...] + MEAN * u_emb
    epad[248:256, :] = jnp.zeros((8, 256), jnp.float32)
    epad[0:ROWS, 0:192] = a_emb[...] - KEEP * m_emb[...] - STEP * u_emb
    et[...] = jnp.transpose(epad[...])[0:192, :].reshape(4, 48, 256)

    def emb_copy(i):
        return pltpu.make_async_remote_copy(
            src_ref=et.at[i], dst_ref=gath.at[f], send_sem=e_ss.at[i], recv_sem=e_rs.at[f],
            device_id={"fsdp": g * 4 + i}, device_id_type=pl.DeviceIdType.MESH)

    plane = lax.div(f, 4)

    @pl.loop(0, 4)
    def _(i):
        @pl.when(f != g * 4 + i)
        def _():
            emb_copy(i).start()

    @pl.when(plane == g)
    def _():
        gath[f] = et[lax.rem(f, 4)]

    each(quarter_copy, G, "wait_recv")
    own_sum[...] = quart_in[0] + quart_in[1] + quart_in[2] + quart_in[3]
    sums[g] = own_sum[...]
    each(sum_copy, G, "start")
    each(sum_copy, G, "wait_recv")
    total = jnp.concatenate([sums[q, 0:144, 0:96] for q in range(G)], axis=0)
    spread = spread_rows()
    umsg[:, :, 0:576] = dot(spread, total, 1, 1).reshape(F, 8, 576)
    urecv[f] = umsg[f]
    each(total_copy, F, "start")

    up = jnp.logical_and(g >= plane, g < G - 1)
    down = jnp.logical_and(g <= plane, g > 0)

    def up_copy(s):
        return pltpu.make_async_remote_copy(
            src_ref=gath.at[s], dst_ref=gath.at[s], send_sem=up_ss.at[s], recv_sem=e_rs.at[s],
            device_id={"rep": jnp.minimum(g + 1, G - 1)}, device_id_type=pl.DeviceIdType.MESH)

    def down_copy(s):
        return pltpu.make_async_remote_copy(
            src_ref=gath.at[s], dst_ref=gath.at[s], send_sem=dn_ss.at[s], recv_sem=e_rs.at[s],
            device_id={"rep": jnp.maximum(g - 1, 0)}, device_id_type=pl.DeviceIdType.MESH)

    @pl.loop(0, F)
    def _(k):
        s = peer_f(k)

        @pl.when(jnp.logical_or(plane != g, s != f))
        def _():
            up_copy(s).wait_recv()

        @pl.when(up)
        def _():
            up_copy(s).start()

        @pl.when(down)
        def _():
            down_copy(s).start()

    each(anchor_copy, F, "wait_recv")
    fixed = dot(arecv[...].reshape(128, 640)[:, 0:576], spread, 0, 0)
    fresh = fixed - STEP * total
    acc = jnp.zeros((48, 384), jnp.float32)
    for q in range(G):
        new_attn[q * 48 : (q + 1) * 48, :] = fresh[q * 144 : q * 144 + 48, :]
        new_out[q * 48 : (q + 1) * 48, :] = fresh[q * 144 + 48 : q * 144 + 96, :]
        acc = acc + dot(fresh[q * 144 + 96 : q * 144 + 144, :], pick_columns(q), 1, 1)
    new_in[...] = acc
    for t in range(F):
        new_small[t : t + 1, :] = arecv[t, 6:7, 0:120] - STEP * own_sum[144 + t : 145 + t, 0:120]
    next_small[...] = MOMENTUM_COEF * m_small[...] + MEAN * own_sum[pl.ds(144 + f, 1), 0:120]

    each(total_copy, F, "wait_recv")
    for t in range(F):
        for q in range(G):
            wide[q, :, t * 48 : (t + 1) * 48] = urecv[t, :, q * 144 : q * 144 + 48]
            widef[:, t * 192 + q * 48 : t * 192 + q * 48 + 48] = urecv[t, :, q * 144 + 48 : q * 144 + 96]
            wide[4 + q, :, t * 48 : (t + 1) * 48] = urecv[t, :, q * 144 + 96 : q * 144 + 144]
    for q in range(G):
        for s in range(6):
            lin[0, pl.ds(q * 6 + s, 6, stride=24), :] = wide[q, 0:6, s * 128 : (s + 1) * 128]
            lin[2, pl.ds(q * 36 + s, 6, stride=6), :] = wide[4 + q, 0:6, s * 128 : (s + 1) * 128]
    for s in range(24):
        lin[1, pl.ds(s, 6, stride=24), :] = widef[0:6, s * 128 : (s + 1) * 128]
    next_attn[...] = MOMENTUM_COEF * m_attn[...] + MEAN * lin[0]
    next_out[...] = MOMENTUM_COEF * m_out[...] + MEAN * lin[1]
    next_in[...] = MOMENTUM_COEF * m_in[...] + MEAN * lin[2]

    for s in range(F):
        new_emb[s * ROWS : (s + 1) * ROWS, :] = jnp.transpose(gath[s])[0:ROWS, :]

    each(left_copy, G, "wait_send")
    each(right_copy, G, "wait_send")
    each(quarter_copy, G, "wait_send")
    each(sum_copy, G, "wait_send")
    each(anchor_copy, F, "wait_send")
    each(total_copy, F, "wait_send")

    @pl.loop(0, 4)
    def _(i):
        @pl.when(f != g * 4 + i)
        def _():
            emb_copy(i).wait_send()

    @pl.loop(0, F)
    def _(s):
        @pl.when(up)
        def _():
            up_copy(s).wait_send()

        @pl.when(down)
        def _():
            down_copy(s).wait_send()


def on_device(
    delta_attn, delta_in, delta_out, delta_small, emb_left, emb_right,
    anchor_attn, anchor_in, anchor_out, anchor_small, anchor_emb,
    moment_attn, moment_in, moment_out, moment_small, moment_emb,
):
    f32 = jnp.float32
    shape = lambda *s: jax.ShapeDtypeStruct(s, f32)
    vmem = pl.BlockSpec(memory_space=pltpu.VMEM)
    buf = lambda *s: pltpu.VMEM(s, f32)
    sem = lambda n: pltpu.SemaphoreType.DMA((n,))
    outs = pl.pallas_call(
        kernel,
        out_shape=(
            shape(192, 96), shape(48, 384), shape(192, 96), shape(16, 120), shape(4016, 48),
            shape(144, 128), shape(144, 128), shape(144, 128), shape(1, 120), shape(251, 192),
        ),
        in_specs=[vmem] * 16,
        out_specs=(vmem,) * 10,
        scratch_shapes=[
            buf(3, 144, 128), buf(8, 8, 768), buf(8, 3072),
            buf(4, 160, 128), buf(4, 160, 128), buf(160, 128), buf(4, 160, 128),
            buf(256, 64), buf(64, 256), buf(4, 64, 256), buf(4, 64, 256), buf(4, 64, 256),
            buf(256, 256), buf(4, 48, 256),
            buf(F, 8, 640), buf(F, 8, 640), buf(F, 8, 640), buf(F, 8, 640), buf(F, 48, 256),
            sem(G), sem(G), sem(G), sem(G), sem(G), sem(G), sem(F), sem(F), sem(G), sem(G), sem(F), sem(F),
            sem(4), sem(F), sem(F), sem(F),
        ],
        compiler_params=pltpu.CompilerParams(collective_id=0, has_side_effects=True, vmem_limit_bytes=48 * 2**20),
        name="outer_step",
    )(
        delta_attn.reshape(192, 96), delta_in[0], delta_out[0], delta_small.reshape(16, 120),
        emb_left[0, 0], emb_right[0],
        anchor_attn.reshape(144, 128), anchor_in.reshape(144, 128), anchor_out.reshape(144, 128),
        anchor_small[None, :], anchor_emb.reshape(251, 192),
        moment_attn.reshape(144, 128), moment_in.reshape(144, 128), moment_out.reshape(144, 128),
        moment_small[None, :], moment_emb.reshape(251, 192),
    )
    return (
        outs[0].reshape(4, 48, 96), outs[1], outs[2], outs[3].reshape(1920), outs[4],
        outs[5].reshape(1, 18432), outs[6].reshape(1, 18432), outs[7].reshape(1, 18432),
        outs[8].reshape(120), outs[9].reshape(1, 1, 1, 48192),
    )


def solution(mesh):
    placed = (
        P("rep", None, "fsdp", "tp"),
        P("rep", "fsdp", "tp"),
        P("rep", "fsdp", "tp"),
        P("rep", None),
        P("rep", "tp", "fsdp", None),
        P("rep", None, None),
        P("tp", "fsdp"),
        P("tp", "fsdp"),
        P("tp", "fsdp"),
        P("fsdp"),
        P("tp", "fsdp", "rep", None),
        P("tp", "fsdp"),
        P("tp", "fsdp"),
        P("tp", "fsdp"),
        P("fsdp"),
        P("tp", "fsdp", "rep", None),
    )
    return jax.shard_map(
        on_device,
        mesh=mesh,
        in_specs=placed,
        out_specs=(
            P(None, "fsdp", "tp"),
            P("fsdp", "tp"),
            P("fsdp", "tp"),
            P(),
            P("tp", "fsdp"),
            P("tp", "fsdp"),
            P("tp", "fsdp"),
            P("tp", "fsdp"),
            P("fsdp"),
            P("tp", "fsdp", "rep", None),
        ),
        check_vma=False,
    )
```

time: 247 us -> 93.5 us (0.38)
  the two profiles are of different devices: /device:TPU:57 before, /device:TPU:317 now
where the time goes in v1:
time: 93.5 us; the launch traced here: 92.8 us
  Pallas kernels  69.4 us (74%)
  local copies, waits for them, and re-layouts  19.1 us (20%)
  other arithmetic  3.56 us (4%)
    pallas_call x1, Pallas kernels, on_device(): pl.pallas_call(kernel, out_shape=(shape(192, 96), shape(48, 384), shape(1...  69.4 us
    unnamed x41, local copies, waits for them, and re-layouts  17.3 us
    unnamed x3, other arithmetic  3.56 us

profile of v1, /device:TPU:317, one launch (start us, length us, event | category | flops | bytes accessed | tf_op | source)
XLA Modules:
  0.0 92.8 jit_solution(3600739663190451533)
XLA Ops:
  0.6 0.0 copy-start
  0.7 0.8 reduce
  1.4 0.1 reshape.72.d_small
  1.5 0.9 %copy.28 = f32[1,1,251,64]{3,2,1,0:T(8,128)S(1)} copy(f32[1,1,251,64]{2,3,1,0:T(8,128)} %param.20) | data formatting | bytes 128512 | tf_op args[4]
  2.4 1.4 %reduce.1 = f32[48192]{0:T(1024)S(1)} reduce(f32[1,1,1,48192]{3,2,1,0:T(1,128)} %param.26, f32[]{:T(128)} %constant.16), dimensions={0,1,2}, to_apply=%param.26.reduce_sub_computation | reduce | bytes 385540 | tf_op args[10]
  3.8 0.1 reshape.76.a_emb
  3.9 1.4 %reduce.2 = f32[48192]{0:T(1024)S(1)} reduce(f32[1,1,1,48192]{3,2,1,0:T(1,128)} %param.31, f32[]{:T(128)} %constant.16), dimensions={0,1,2}, to_apply=%param.31.reduce_sub_computation | reduce | bytes 385540 | tf_op args[15]
  5.3 0.1 reshape.80.m_emb
  5.4 0.0 copy-done
  5.5 0.0 copy-start.1
  5.5 0.9 copy-done.1
  6.3 0.0 copy-start.2
  6.4 0.9 copy-done.2
  7.2 0.0 copy-start.7
  7.2 0.9 copy-done.7
  8.1 0.0 copy-start.8
  8.1 0.9 copy-done.8
  9.0 0.0 copy-start.9
  9.0 0.9 copy-done.9
  9.9 0.0 copy-start.10
  9.9 0.9 copy-done.10
  10.8 0.0 copy-start.11
  10.8 0.9 copy-done.11
  11.7 0.0 copy-start.12
  11.7 0.9 copy-done.12
  12.6 0.0 copy-start.13
  12.6 0.9 copy-done.13
  13.4 0.0 copy-start.14
  13.4 0.7 copy-done.14
  14.1 0.0 copy-start.15
  14.1 0.7 copy-done.15
  14.7 69.4 %outer_step.1 = (f32[192,96]{1,0:T(8,128)S(1)}, f32[48,384]{1,0:T(8,128)S(1)}, f32[192,96]{1,0:T(8,128)S(1)}, f32[16,120]{1,0:T(8,128)S(1)}, f32[4016,48]{1,0:T(...) custom-call(f32[192,96]{1,0:T(8,128)S(1)} %bitcast.21, ...), custom_call_target="tpu_custom_call" | custom-call | tf_op jit(solution)/shard_map/outer_step/pallas_call | solution.py:282
  84.2 0.0 copy-start.3
  84.2 0.6 copy-done.3
  84.8 0.0 copy-start.5
  84.8 0.6 copy-done.5
  85.5 0.7 reshape.82
  86.1 0.9 reshape.87
  87.1 1.5 %copy.29 = f32[4016,48]{0,1:T(8,128)} copy(f32[4016,48]{1,0:T(8,128)S(1)} %get-tuple-element.44) | data formatting | bytes 1542144
  88.5 0.6 copy.37
  89.2 0.0 copy-done.6
  89.2 0.6 copy.38
  89.8 0.6 copy.39
  90.4 0.0 copy-done.4
  90.4 0.6 copy.40
  91.1 0.6 copy.41
  91.7 0.6 copy.42
  92.3 0.5 copy.43
  (2 shorter events, 0.0 us)
Async XLA Ops:
  0.6 4.8 %copy-start = (f32[1,64,768]{2,1,0:T(8,128)S(1)}, f32[1,64,768]{2,1,0:T(8,128)}, u32[]{:S(2)}) copy-start(f32[1,64,768]{2,1,0:T(8,128)} %param.21) | copy-start | bytes 589828
  5.5 0.9 copy-start.1
  6.3 0.9 copy-start.2
  7.2 0.9 copy-start.7
  8.1 0.9 copy-start.8
  9.0 0.9 copy-start.9
  9.9 0.9 copy-start.10
  10.8 0.9 copy-start.11
  11.7 0.9 copy-start.12
  12.6 0.9 copy-start.13
  13.4 0.7 copy-start.14
  14.1 0.7 copy-start.15
  84.2 0.6 copy-start.3
  84.8 0.6 copy-start.5
  85.5 3.7 %copy-start.6 = (f32[48,384]{1,0:T(8,128)S(1)}, f32[48,384]{1,0:T(8,128)}, u32[]{:S(2)}) copy-start(f32[48,384]{1,0:T(8,128)} %copy-done.5) | copy-start | bytes 221188
  85.5 5.0 %copy-start.4 = (f32[144,128]{1,0:T(8,128)S(1)}, f32[144,128]{1,0:T(8,128)}, u32[]{:S(2)}) copy-start(f32[144,128]{1,0:T(8,128)} %copy-done.3) | copy-start | bytes 221188

commit v2 on v1

--- a/solution.py
+++ b/solution.py
@@ -38,23 +38,49 @@
 
 
 def kernel(
-    d_attn, d_in, d_out, d_small, left, right,
+    d_attn_h, d_in_h, d_out_h, d_small_h, left_h, right_h,
+    a_attn_h, a_in_h, a_out_h, a_small_h, a_emb_h,
+    m_attn_h, m_in_h, m_out_h, m_small_h, m_emb_h,
+    new_attn_h, new_in_h, new_out_h, new_small_h, new_emb_h,
+    next_attn_h, next_in_h, next_out_h, next_small_h, next_emb_h,
+    new_attn, new_in, new_out, new_small, new_emb,
+    next_attn, next_in, next_out, next_small, next_emb,
+    d_attn, d_in, d_out, d_small, right,
     a_attn, a_in, a_out, a_small, a_emb,
     m_attn, m_in, m_out, m_small, m_emb,
-    new_attn, new_in, new_out, new_small, new_emb,
-    next_attn, next_in, next_out, next_small, next_emb,
-    lin, wide, widef, quart, quart_in, own_sum, sums, lpad, lt_own, lts, rts_own, rts, epad, et,
+    flat_small, lin, wide, widef, quart, quart_in, own_sum, sums, tot, lts, rts_own, rts, base, un, et,
     amsg, arecv, umsg, urecv, gath,
-    q_ss, q_rs, l_ss, l_rs, r_ss, r_rs, a_ss, a_rs, s_ss, s_rs, u_ss, u_rs, e_ss, up_ss, dn_ss, e_rs,
+    in_s, out_s, q_ss, q_rs, l_ss, l_rs, r_ss, r_rs, x_ss, x_rs, a_ss, a_rs, s_ss, s_rs, u_ss, u_rs, e_ss, up_ss, dn_ss, e_rs,
 ):
     f = lax.axis_index("fsdp")
     g = lax.axis_index("rep")
+    c = lax.rem(f, 2)
 
     def peer_f(d):
         return lax.rem(f + d, F)
 
     def peer_g(d):
         return lax.rem(g + d, G)
+
+    loads = [
+        pltpu.make_async_copy(src, dst, in_s.at[i])
+        for i, (src, dst) in enumerate((
+            (left_h, lts.at[g]), (right_h, right), (d_in_h, d_in), (d_attn_h, d_attn), (d_out_h, d_out),
+            (d_small_h, d_small), (a_attn_h, a_attn), (m_attn_h, m_attn), (a_out_h, a_out), (m_out_h, m_out),
+            (a_in_h, a_in), (m_in_h, m_in), (a_small_h, a_small), (m_small_h, m_small), (a_emb_h, a_emb),
+            (m_emb_h, m_emb),
+        ))
+    ]
+    for load in loads:
+        load.start()
+    stores = [
+        pltpu.make_async_copy(src, dst, out_s.at[i])
+        for i, (src, dst) in enumerate((
+            (new_attn, new_attn_h), (new_in, new_in_h), (new_out, new_out_h), (new_small, new_small_h),
+            (new_emb, new_emb_h), (next_attn, next_attn_h), (next_in, next_in_h), (next_out, next_out_h),
+            (next_small, next_small_h), (next_emb, next_emb_h),
+        ))
+    ]
 
     bar = pltpu.get_barrier_semaphore()
 
@@ -66,45 +92,53 @@
     def _(d):
         pl.semaphore_signal(bar, inc=1, device_id={"rep": peer_g(d)}, device_id_type=pl.DeviceIdType.MESH)
 
-    lpad[pl.ds(248, 8), :] = jnp.zeros((8, 64), jnp.float32)
-    lpad[pl.ds(0, ROWS), :] = left[...]
-    eye = (lax.broadcasted_iota(jnp.int32, (64, 64), 0) == lax.broadcasted_iota(jnp.int32, (64, 64), 1)).astype(jnp.float32)
-    lt_own[...] = dot(eye, lpad[...], 1, 1)
-    lts[g] = lt_own[...]
-    for q in range(G):
-        rts_own[q, :, 0:192] = right[:, q * 192 : (q + 1) * 192]
+    for load in loads[:6]:
+        load.wait()
+    for q in range(G):
+        for h in range(2):
+            rts_own[q, h, :, 0:192] = right[h * 32 : (h + 1) * 32, q * 192 : (q + 1) * 192]
     rts[g] = rts_own[g]
 
-    small = d_small[...]
+    for t in range(F):
+        quart[0, 112 + t : 113 + t, 0:120] = d_small[:, t * 120 : (t + 1) * 120]
+    small = quart[0, 112:128, 0:120]
     x_in = d_in[...]
     for q in range(G):
+        x_q = dot(x_in, pick_columns(q), 1, 0)
         quart[q, 0:48, 0:96] = d_attn[q * 48 : (q + 1) * 48, :]
+        quart[q, 0:48, 96:128] = x_q[:, 0:32]
         quart[q, 48:96, 0:96] = d_out[q * 48 : (q + 1) * 48, :]
-        quart[q, 96:144, 0:96] = dot(x_in, pick_columns(q), 1, 0)
-        quart[q, 144:160, 0:120] = small
+        quart[q, 48:96, 96:128] = x_q[:, 32:64]
+        for b in range(3):
+            quart[q, 96:112, b * 32 : (b + 1) * 32] = x_q[b * 16 : (b + 1) * 16, 64:96]
+        if q:
+            quart[q, 112:128, 0:120] = small
     quart_in[g] = quart[g]
 
     pl.semaphore_wait(bar, F + G - 2)
 
+    def rep_copy(src, dst, ss, rs, d):
+        return pltpu.make_async_remote_copy(
+            src_ref=src, dst_ref=dst, send_sem=ss.at[d], recv_sem=rs.at[d],
+            device_id={"rep": peer_g(d)}, device_id_type=pl.DeviceIdType.MESH)
+
     def left_copy(d):
-        return pltpu.make_async_remote_copy(
-            src_ref=lt_own, dst_ref=lts.at[g], send_sem=l_ss.at[d], recv_sem=l_rs.at[d],
-            device_id={"rep": peer_g(d)}, device_id_type=pl.DeviceIdType.MESH)
+        return rep_copy(lts.at[g], lts.at[g], l_ss, l_rs, d)
 
     def right_copy(d):
-        return pltpu.make_async_remote_copy(
-            src_ref=rts_own.at[peer_g(d)], dst_ref=rts.at[g], send_sem=r_ss.at[d], recv_sem=r_rs.at[d],
-            device_id={"rep": peer_g(d)}, device_id_type=pl.DeviceIdType.MESH)
+        return rep_copy(rts_own.at[peer_g(d), c], rts.at[g, c], r_ss, r_rs, d)
 
     def quarter_copy(d):
-        return pltpu.make_async_remote_copy(
-            src_ref=quart.at[peer_g(d)], dst_ref=quart_in.at[g], send_sem=q_ss.at[d], recv_sem=q_rs.at[d],
-            device_id={"rep": peer_g(d)}, device_id_type=pl.DeviceIdType.MESH)
+        return rep_copy(quart.at[peer_g(d)], quart_in.at[g], q_ss, q_rs, d)
 
     def sum_copy(d):
-        return pltpu.make_async_remote_copy(
-            src_ref=own_sum, dst_ref=sums.at[g], send_sem=s_ss.at[d], recv_sem=s_rs.at[d],
-            device_id={"rep": peer_g(d)}, device_id_type=pl.DeviceIdType.MESH)
+        return rep_copy(own_sum.at[pl.ds(0, 112)], sums.at[g], s_ss, s_rs, d)
+
+    def half_copy(d):
+        part = rts.at[peer_g(G - d), c]
+        return pltpu.make_async_remote_copy(
+            src_ref=part, dst_ref=part, send_sem=x_ss.at[d], recv_sem=x_rs.at[d],
+            device_id={"fsdp": f + 1 - 2 * c}, device_id_type=pl.DeviceIdType.MESH)
 
     def anchor_copy(d):
         return pltpu.make_async_remote_copy(
@@ -121,9 +155,26 @@
         def _(d):
             getattr(copy(d), what)()
 
+    each(right_copy, G, "start")
     each(left_copy, G, "start")
-    each(right_copy, G, "start")
     each(quarter_copy, G, "start")
+
+    for load in loads[6:]:
+        load.wait()
+
+    @pl.loop(0, 125, unroll=5)
+    def _(p):
+        at = pl.ds(pl.multiple_of(p * 384, 128), 384)
+        x = a_emb[:, at] - KEEP * m_emb[:, at]
+        base[pl.ds(2 * p, 1), 0:192] = x[:, 0:192]
+        base[pl.ds(2 * p + 1, 1), 0:192] = x[:, 192:384]
+
+    base[250:251, 0:192] = a_emb[:, 48000:48192] - KEEP * m_emb[:, 48000:48192]
+
+    @pl.loop(1, G)
+    def _(d):
+        right_copy(d).wait_recv()
+        half_copy(d).start()
 
     amsg[...] = jnp.zeros((F, 8, 640), jnp.float32)
     lin[0] = a_attn[...] - KEEP * m_attn[...]
@@ -146,15 +197,11 @@
     each(anchor_copy, F, "start")
 
     each(left_copy, G, "wait_recv")
-    each(right_copy, G, "wait_recv")
-    u_emb = dot(lts[0], rts[0, :, 0:192], 0, 0)
-    for k in range(1, G):
-        u_emb = u_emb + dot(lts[k], rts[k, :, 0:192], 0, 0)
-    u_emb = u_emb[0:ROWS, :]
-    next_emb[...] = MOMENTUM_COEF * m_emb[...] + MEAN * u_emb
-    epad[248:256, :] = jnp.zeros((8, 256), jnp.float32)
-    epad[0:ROWS, 0:192] = a_emb[...] - KEEP * m_emb[...] - STEP * u_emb
-    et[...] = jnp.transpose(epad[...])[0:192, :].reshape(4, 48, 256)
+    each(half_copy, G, "wait_recv")
+    u_emb = dot(lts[...].reshape(256, ROWS), rts[...].reshape(256, 256)[:, 0:192], 0, 0)
+    un[0:ROWS, 0:192] = u_emb
+    base[0:ROWS, 0:192] = base[0:ROWS, 0:192] - STEP * u_emb
+    et[...] = jnp.transpose(base[...])[0:192, 0:ROWS].reshape(4, 48, ROWS)
 
     def emb_copy(i):
         return pltpu.make_async_remote_copy(
@@ -175,10 +222,26 @@
 
     each(quarter_copy, G, "wait_recv")
     own_sum[...] = quart_in[0] + quart_in[1] + quart_in[2] + quart_in[3]
-    sums[g] = own_sum[...]
+    sums[g] = own_sum[0:112, :]
     each(sum_copy, G, "start")
+
+    @pl.loop(0, 125, unroll=5)
+    def _(p):
+        at = pl.ds(pl.multiple_of(p * 384, 128), 384)
+        x = jnp.concatenate([un[pl.ds(2 * p, 1), 0:192], un[pl.ds(2 * p + 1, 1), 0:192]], axis=1)
+        next_emb[:, at] = MOMENTUM_COEF * m_emb[:, at] + MEAN * x
+
+    next_emb[:, 48000:48192] = MOMENTUM_COEF * m_emb[:, 48000:48192] + MEAN * un[250:251, 0:192]
+    stores[9].start()
+
     each(sum_copy, G, "wait_recv")
-    total = jnp.concatenate([sums[q, 0:144, 0:96] for q in range(G)], axis=0)
+    for q in range(G):
+        tot[q, 0:96, 0:96] = sums[q, 0:96, 0:96]
+        tot[q, 96:144, 0:32] = sums[q, 0:48, 96:128]
+        tot[q, 96:144, 32:64] = sums[q, 48:96, 96:128]
+        for b in range(3):
+            tot[q, 96 + b * 16 : 112 + b * 16, 64:96] = sums[q, 96:112, b * 32 : (b + 1) * 32]
+    total = tot[...].reshape(576, 128)[:, 0:96]
     spread = spread_rows()
     umsg[:, :, 0:576] = dot(spread, total, 1, 1).reshape(F, 8, 576)
     urecv[f] = umsg[f]
@@ -197,21 +260,24 @@
             src_ref=gath.at[s], dst_ref=gath.at[s], send_sem=dn_ss.at[s], recv_sem=e_rs.at[s],
             device_id={"rep": jnp.maximum(g - 1, 0)}, device_id_type=pl.DeviceIdType.MESH)
 
-    @pl.loop(0, F)
-    def _(k):
-        s = peer_f(k)
-
-        @pl.when(jnp.logical_or(plane != g, s != f))
-        def _():
-            up_copy(s).wait_recv()
-
-        @pl.when(up)
-        def _():
-            up_copy(s).start()
-
-        @pl.when(down)
-        def _():
-            down_copy(s).start()
+    def relay(lo, hi):
+        @pl.loop(lo, hi)
+        def _(k):
+            s = peer_f(k)
+
+            @pl.when(jnp.logical_or(plane != g, s != f))
+            def _():
+                up_copy(s).wait_recv()
+
+            @pl.when(up)
+            def _():
+                up_copy(s).start()
+
+            @pl.when(down)
+            def _():
+                down_copy(s).start()
+
+    relay(0, 6)
 
     each(anchor_copy, F, "wait_recv")
     fixed = dot(arecv[...].reshape(128, 640)[:, 0:576], spread, 0, 0)
@@ -223,8 +289,14 @@
         acc = acc + dot(fresh[q * 144 + 96 : q * 144 + 144, :], pick_columns(q), 1, 1)
     new_in[...] = acc
     for t in range(F):
-        new_small[t : t + 1, :] = arecv[t, 6:7, 0:120] - STEP * own_sum[144 + t : 145 + t, 0:120]
-    next_small[...] = MOMENTUM_COEF * m_small[...] + MEAN * own_sum[pl.ds(144 + f, 1), 0:120]
+        flat_small[:, t * 120 : (t + 1) * 120] = arecv[t, 6:7, 0:120] - STEP * own_sum[112 + t : 113 + t, 0:120]
+    for t in range(15):
+        new_small[t : t + 1, :] = flat_small[:, t * 128 : (t + 1) * 128]
+    next_small[...] = MOMENTUM_COEF * m_small[...] + MEAN * own_sum[pl.ds(112 + f, 1), 0:120]
+    for i in (0, 1, 2, 3, 8):
+        stores[i].start()
+
+    relay(6, 11)
 
     each(total_copy, F, "wait_recv")
     for t in range(F):
@@ -241,12 +313,17 @@
     next_attn[...] = MOMENTUM_COEF * m_attn[...] + MEAN * lin[0]
     next_out[...] = MOMENTUM_COEF * m_out[...] + MEAN * lin[1]
     next_in[...] = MOMENTUM_COEF * m_in[...] + MEAN * lin[2]
-
+    for i in (5, 6, 7):
+        stores[i].start()
+
+    relay(11, F)
     for s in range(F):
-        new_emb[s * ROWS : (s + 1) * ROWS, :] = jnp.transpose(gath[s])[0:ROWS, :]
+        new_emb[:, s * ROWS : (s + 1) * ROWS] = gath[s]
+    stores[4].start()
 
     each(left_copy, G, "wait_send")
     each(right_copy, G, "wait_send")
+    each(half_copy, G, "wait_send")
     each(quarter_copy, G, "wait_send")
     each(sum_copy, G, "wait_send")
     each(anchor_copy, F, "wait_send")
@@ -267,6 +344,23 @@
         @pl.when(down)
         def _():
             down_copy(s).wait_send()
+
+    for store in stores:
+        store.wait()
+
+
+def write_out(*refs):
+    n = (len(refs) - 2) // 3
+    took, gave = refs[3 * n], refs[3 * n + 1]
+    inward = [pltpu.make_async_copy(refs[i], refs[2 * n + i], took.at[i]) for i in range(n)]
+    outward = [pltpu.make_async_copy(refs[2 * n + i], refs[n + i], gave.at[i]) for i in range(n)]
+    for copy in inward:
+        copy.start()
+    for i in range(n):
+        inward[i].wait()
+        outward[i].start()
+    for copy in outward:
+        copy.wait()
 
 
 def on_device(
@@ -276,38 +370,51 @@
 ):
     f32 = jnp.float32
     shape = lambda *s: jax.ShapeDtypeStruct(s, f32)
-    vmem = pl.BlockSpec(memory_space=pltpu.VMEM)
+    hbm = pl.BlockSpec(memory_space=pltpu.HBM)
     buf = lambda *s: pltpu.VMEM(s, f32)
     sem = lambda n: pltpu.SemaphoreType.DMA((n,))
-    outs = pl.pallas_call(
+    results = (
+        shape(192, 96), shape(48, 384), shape(192, 96), shape(15, 128), shape(48, 4016),
+        shape(144, 128), shape(144, 128), shape(144, 128), shape(1, 120), shape(1, 48192),
+    )
+    held = pl.pallas_call(
         kernel,
-        out_shape=(
-            shape(192, 96), shape(48, 384), shape(192, 96), shape(16, 120), shape(4016, 48),
-            shape(144, 128), shape(144, 128), shape(144, 128), shape(1, 120), shape(251, 192),
-        ),
-        in_specs=[vmem] * 16,
-        out_specs=(vmem,) * 10,
+        out_shape=results,
+        in_specs=[hbm] * 16,
+        out_specs=(hbm,) * 10,
         scratch_shapes=[
-            buf(3, 144, 128), buf(8, 8, 768), buf(8, 3072),
-            buf(4, 160, 128), buf(4, 160, 128), buf(160, 128), buf(4, 160, 128),
-            buf(256, 64), buf(64, 256), buf(4, 64, 256), buf(4, 64, 256), buf(4, 64, 256),
-            buf(256, 256), buf(4, 48, 256),
-            buf(F, 8, 640), buf(F, 8, 640), buf(F, 8, 640), buf(F, 8, 640), buf(F, 48, 256),
-            sem(G), sem(G), sem(G), sem(G), sem(G), sem(G), sem(F), sem(F), sem(G), sem(G), sem(F), sem(F),
-            sem(4), sem(F), sem(F), sem(F),
+            *(pltpu.VMEM(r.shape, f32) for r in results),
+            buf(192, 96), buf(48, 384), buf(192, 96), buf(1, 1920), buf(64, 768),
+            buf(144, 128), buf(144, 128), buf(144, 128), buf(1, 120), buf(1, 48192),
+            buf(144, 128), buf(144, 128), buf(144, 128), buf(1, 120), buf(1, 48192),
+            buf(1, 1920), buf(3, 144, 128), buf(8, 8, 768), buf(8, 3072),
+            buf(4, 128, 128), buf(4, 128, 128), buf(128, 128), buf(4, 112, 128), buf(4, 144, 128),
+            buf(4, 64, ROWS), buf(4, 2, 32, 256), buf(4, 2, 32, 256),
+            buf(256, 256), buf(256, 256), buf(4, 48, ROWS),
+            buf(F, 8, 640), buf(F, 8, 640), buf(F, 8, 640), buf(F, 8, 640), buf(F, 48, ROWS),
+            sem(16), sem(10), sem(G), sem(G), sem(G), sem(G), sem(G), sem(G), sem(G), sem(G), sem(F), sem(F), sem(G), sem(G),
+            sem(F), sem(F), sem(4), sem(F), sem(F), sem(F),
         ],
-        compiler_params=pltpu.CompilerParams(collective_id=0, has_side_effects=True, vmem_limit_bytes=48 * 2**20),
+        compiler_params=pltpu.CompilerParams(collective_id=0, has_side_effects=True, vmem_limit_bytes=60 * 2**20),
         name="outer_step",
     )(
-        delta_attn.reshape(192, 96), delta_in[0], delta_out[0], delta_small.reshape(16, 120),
-        emb_left[0, 0], emb_right[0],
+        delta_attn.reshape(192, 96), delta_in[0], delta_out[0], delta_small, emb_left[0, 0].T, emb_right[0],
         anchor_attn.reshape(144, 128), anchor_in.reshape(144, 128), anchor_out.reshape(144, 128),
-        anchor_small[None, :], anchor_emb.reshape(251, 192),
+        anchor_small.reshape(1, 120), anchor_emb.reshape(1, 48192),
         moment_attn.reshape(144, 128), moment_in.reshape(144, 128), moment_out.reshape(144, 128),
-        moment_small[None, :], moment_emb.reshape(251, 192),
-    )
+        moment_small.reshape(1, 120), moment_emb.reshape(1, 48192),
+    )
+    outs = pl.pallas_call(
+        write_out,
+        out_shape=results,
+        in_specs=[hbm] * 10,
+        out_specs=(hbm,) * 10,
+        scratch_shapes=[*(pltpu.VMEM(r.shape, f32) for r in results), sem(10), sem(10)],
+        compiler_params=pltpu.CompilerParams(vmem_limit_bytes=60 * 2**20),
+        name="write_out",
+    )(*held)
     return (
-        outs[0].reshape(4, 48, 96), outs[1], outs[2], outs[3].reshape(1920), outs[4],
+        outs[0].reshape(4, 48, 96), outs[1], outs[2], outs[3].reshape(1920), outs[4].T,
         outs[5].reshape(1, 18432), outs[6].reshape(1, 18432), outs[7].reshape(1, 18432),
         outs[8].reshape(120), outs[9].reshape(1, 1, 1, 48192),
     )

time: 93.5 us -> 68.8 us (0.74)
  local copies, waits for them, and re-layouts: 19.1 us -> 0 us
  other arithmetic: 3.56 us -> 0 us
  Pallas kernels: 69.4 us -> 68 us
    unnamed x41 -> x0, local copies, waits for them, and re-layouts: 17.3 us -> none
    unnamed x3 -> x0, other arithmetic: 3.56 us -> none
    reshape x5 -> x0, local copies, waits for them, and re-layouts: 1.88 us -> none  [the longest x1 0.91 us: on_device(): outs[9].reshape(1, 1, 1, 48192)]
    pallas_call x1 -> x2, Pallas kernels: 69.4 us -> 68 us  [the longest x1 65.5 us: on_device(): pl.pallas_call(kernel, out_shape=results, in_specs=[hbm] * 16, out_specs=...]
where the time goes in v2:
time: 68.8 us; the launch traced here: 68.6 us
  Pallas kernels  68 us (99%)
    pallas_call x1, Pallas kernels, on_device(): pl.pallas_call(kernel, out_shape=results, in_specs=[hbm] * 16, out_specs=...  65.5 us
    pallas_call x1, Pallas kernels, on_device(): pl.pallas_call(write_out, out_shape=results, in_specs=[hbm] * 10, out_spe...  2.49 us

profile of v2, /device:TPU:317, one launch (start us, length us, event | category | flops | bytes accessed | tf_op | source)
XLA Modules:
  0.0 68.6 jit_solution(3761969438734178111)
XLA Ops:
  0.6 65.5 %outer_step.1 = (f32[192,96]{1,0:T(8,128)}, f32[48,384]{1,0:T(8,128)}, f32[192,96]{1,0:T(8,128)}, f32[15,128]{1,0:T(8,128)}, f32[48,4016]{1,0:T(8,128)}, /*index...) custom-call(f32[192,96]{1,0:T(8,128)} %bitcast.28, ...), custom_call_target="tpu_custom_call" | custom-call | tf_op jit(solution)/shard_map/outer_step/pallas_call | solution.py:380
  66.1 2.5 %write_out.1 = (f32[192,96]{1,0:T(8,128)}, f32[48,384]{1,0:T(8,128)}, f32[192,96]{1,0:T(8,128)}, f32[15,128]{1,0:T(8,128)}, f32[48,4016]{1,0:T(8,128)}, /*index=...) custom-call(f32[192,96]{1,0:T(8,128)} %get-tuple-element.30.refs_0_, ...), custom_call_target="tpu_custom_call" | custom-call | tf_op jit(solution)/shard_map/write_out/pallas_call | solution.py:407

commit v3 on v2

--- a/solution.py
+++ b/solution.py
@@ -50,11 +50,14 @@
     m_attn, m_in, m_out, m_small, m_emb,
     flat_small, lin, wide, widef, quart, quart_in, own_sum, sums, tot, lts, rts_own, rts, base, un, et,
     amsg, arecv, umsg, urecv, gath,
-    in_s, out_s, q_ss, q_rs, l_ss, l_rs, r_ss, r_rs, x_ss, x_rs, a_ss, a_rs, s_ss, s_rs, u_ss, u_rs, e_ss, up_ss, dn_ss, e_rs,
+    in_s, out_s, q_ss, q_rs, lu_ss, ld_ss, l_rs, r_ss, r_rs, x_ss, x_rs, a_ss, a_rs, su_ss, sd_ss, s_rs, u_ss, u_rs, e_ss, up_ss, dn_ss, e_rs,
 ):
     f = lax.axis_index("fsdp")
     g = lax.axis_index("rep")
+    tp = lax.axis_index("tp")
     c = lax.rem(f, 2)
+    x = lax.rem(tp, 4)
+    part = 2 * x + c
 
     def peer_f(d):
         return lax.rem(f + d, F)
@@ -92,12 +95,109 @@
     def _(d):
         pl.semaphore_signal(bar, inc=1, device_id={"rep": peer_g(d)}, device_id_type=pl.DeviceIdType.MESH)
 
-    for load in loads[:6]:
+    def near(n):
+        return {"tp": tp - x + lax.rem(x + n // 2, 4), "fsdp": f if n % 2 == 0 else f + 1 - 2 * c}
+
+    for n in range(2, 8):
+        pl.semaphore_signal(bar, inc=1, device_id=near(n), device_id_type=pl.DeviceIdType.MESH)
+
+    for load in loads[:2]:
         load.wait()
     for q in range(G):
-        for h in range(2):
-            rts_own[q, h, :, 0:192] = right[h * 32 : (h + 1) * 32, q * 192 : (q + 1) * 192]
-    rts[g] = rts_own[g]
+        for h in range(8):
+            rts_own[q, h, :, 0:192] = right[h * 8 : (h + 1) * 8, q * 192 : (q + 1) * 192]
+    rts[part, g] = rts_own[g, part]
+
+    pl.semaphore_wait(bar, F + G + 4)
+
+    def rep_copy(src, dst, ss, rs, d):
+        return pltpu.make_async_remote_copy(
+            src_ref=src, dst_ref=dst, send_sem=ss.at[d], recv_sem=rs.at[d],
+            device_id={"rep": peer_g(d)}, device_id_type=pl.DeviceIdType.MESH)
+
+    def right_copy(d):
+        return rep_copy(rts_own.at[peer_g(d), part], rts.at[part, g], r_ss, r_rs, d)
+
+    def line(blocks, up_ss, down_ss, rs):
+        def hop(k, step):
+            ss = up_ss if step > 0 else down_ss
+            return pltpu.make_async_remote_copy(
+                src_ref=blocks.at[k], dst_ref=blocks.at[k], send_sem=ss.at[k], recv_sem=rs.at[k],
+                device_id={"rep": jnp.clip(g + step, 0, G - 1)}, device_id_type=pl.DeviceIdType.MESH)
+
+        def own():
+            @pl.when(g < G - 1)
+            def _():
+                hop(g, 1).start()
+
+            @pl.when(g > 0)
+            def _():
+                hop(g, -1).start()
+
+        def pass_on(d):
+            low = jnp.maximum(g - d, 0)
+            high = jnp.minimum(g + d, G - 1)
+
+            @pl.when(g >= d)
+            def _():
+                hop(low, 1).wait_recv()
+
+                @pl.when(g < G - 1)
+                def _():
+                    hop(low, 1).start()
+
+            @pl.when(g + d < G)
+            def _():
+                hop(high, -1).wait_recv()
+
+                @pl.when(g > 0)
+                def _():
+                    hop(high, -1).start()
+
+        def wait_send():
+            @pl.loop(0, G)
+            def _(k):
+                @pl.when(jnp.logical_and(k <= g, g < G - 1))
+                def _():
+                    hop(k, 1).wait_send()
+
+                @pl.when(jnp.logical_and(k >= g, g > 0))
+                def _():
+                    hop(k, -1).wait_send()
+
+        return own, pass_on, wait_send
+
+    left_own, left_pass, left_wait_send = line(lts, lu_ss, ld_ss, l_rs)
+    sums_own, sums_pass, sums_wait_send = line(sums, su_ss, sd_ss, s_rs)
+
+    def quarter_copy(d):
+        return rep_copy(quart.at[peer_g(d)], quart_in.at[g], q_ss, q_rs, d)
+
+    def near_copy(n):
+        return pltpu.make_async_remote_copy(
+            src_ref=rts.at[part], dst_ref=rts.at[part], send_sem=x_ss.at[n], recv_sem=x_rs.at[n],
+            device_id=near(n), device_id_type=pl.DeviceIdType.MESH)
+
+    def anchor_copy(d):
+        return pltpu.make_async_remote_copy(
+            src_ref=amsg.at[peer_f(d)], dst_ref=arecv.at[f], send_sem=a_ss.at[d], recv_sem=a_rs.at[d],
+            device_id={"fsdp": peer_f(d)}, device_id_type=pl.DeviceIdType.MESH)
+
+    def total_copy(d):
+        return pltpu.make_async_remote_copy(
+            src_ref=umsg.at[peer_f(d)], dst_ref=urecv.at[f], send_sem=u_ss.at[d], recv_sem=u_rs.at[d],
+            device_id={"fsdp": peer_f(d)}, device_id_type=pl.DeviceIdType.MESH)
+
+    def each(copy, n, what):
+        @pl.loop(1, n)
+        def _(d):
+            getattr(copy(d), what)()
+
+    each(right_copy, G, "start")
+    left_own()
+
+    for load in loads[2:6]:
+        load.wait()
 
     for t in range(F):
         quart[0, 112 + t : 113 + t, 0:120] = d_small[:, t * 120 : (t + 1) * 120]
@@ -115,48 +215,10 @@
             quart[q, 112:128, 0:120] = small
     quart_in[g] = quart[g]
 
-    pl.semaphore_wait(bar, F + G - 2)
-
-    def rep_copy(src, dst, ss, rs, d):
-        return pltpu.make_async_remote_copy(
-            src_ref=src, dst_ref=dst, send_sem=ss.at[d], recv_sem=rs.at[d],
-            device_id={"rep": peer_g(d)}, device_id_type=pl.DeviceIdType.MESH)
-
-    def left_copy(d):
-        return rep_copy(lts.at[g], lts.at[g], l_ss, l_rs, d)
-
-    def right_copy(d):
-        return rep_copy(rts_own.at[peer_g(d), c], rts.at[g, c], r_ss, r_rs, d)
-
-    def quarter_copy(d):
-        return rep_copy(quart.at[peer_g(d)], quart_in.at[g], q_ss, q_rs, d)
-
-    def sum_copy(d):
-        return rep_copy(own_sum.at[pl.ds(0, 112)], sums.at[g], s_ss, s_rs, d)
-
-    def half_copy(d):
-        part = rts.at[peer_g(G - d), c]
-        return pltpu.make_async_remote_copy(
-            src_ref=part, dst_ref=part, send_sem=x_ss.at[d], recv_sem=x_rs.at[d],
-            device_id={"fsdp": f + 1 - 2 * c}, device_id_type=pl.DeviceIdType.MESH)
-
-    def anchor_copy(d):
-        return pltpu.make_async_remote_copy(
-            src_ref=amsg.at[peer_f(d)], dst_ref=arecv.at[f], send_sem=a_ss.at[d], recv_sem=a_rs.at[d],
-            device_id={"fsdp": peer_f(d)}, device_id_type=pl.DeviceIdType.MESH)
-
-    def total_copy(d):
-        return pltpu.make_async_remote_copy(
-            src_ref=umsg.at[peer_f(d)], dst_ref=urecv.at[f], send_sem=u_ss.at[d], recv_sem=u_rs.at[d],
-            device_id={"fsdp": peer_f(d)}, device_id_type=pl.DeviceIdType.MESH)
-
-    def each(copy, n, what):
-        @pl.loop(1, n)
-        def _(d):
-            getattr(copy(d), what)()
-
-    each(right_copy, G, "start")
-    each(left_copy, G, "start")
+    left_pass(1)
+    each(right_copy, G, "wait_recv")
+    for n in range(1, 8):
+        near_copy(n).start()
     each(quarter_copy, G, "start")
 
     for load in loads[6:]:
@@ -171,10 +233,7 @@
 
     base[250:251, 0:192] = a_emb[:, 48000:48192] - KEEP * m_emb[:, 48000:48192]
 
-    @pl.loop(1, G)
-    def _(d):
-        right_copy(d).wait_recv()
-        half_copy(d).start()
+    left_pass(2)
 
     amsg[...] = jnp.zeros((F, 8, 640), jnp.float32)
     lin[0] = a_attn[...] - KEEP * m_attn[...]
@@ -196,9 +255,11 @@
     arecv[f] = amsg[f]
     each(anchor_copy, F, "start")
 
-    each(left_copy, G, "wait_recv")
-    each(half_copy, G, "wait_recv")
-    u_emb = dot(lts[...].reshape(256, ROWS), rts[...].reshape(256, 256)[:, 0:192], 0, 0)
+    left_pass(3)
+    for n in range(1, 8):
+        near_copy(n).wait_recv()
+    rhs = jnp.concatenate([rts[:, k, :, :].reshape(64, 256) for k in range(G)], axis=0)
+    u_emb = dot(lts[...].reshape(256, ROWS), rhs[:, 0:192], 0, 0)
     un[0:ROWS, 0:192] = u_emb
     base[0:ROWS, 0:192] = base[0:ROWS, 0:192] - STEP * u_emb
     et[...] = jnp.transpose(base[...])[0:192, 0:ROWS].reshape(4, 48, ROWS)
@@ -223,7 +284,7 @@
     each(quarter_copy, G, "wait_recv")
     own_sum[...] = quart_in[0] + quart_in[1] + quart_in[2] + quart_in[3]
     sums[g] = own_sum[0:112, :]
-    each(sum_copy, G, "start")
+    sums_own()
 
     @pl.loop(0, 125, unroll=5)
     def _(p):
@@ -234,7 +295,8 @@
     next_emb[:, 48000:48192] = MOMENTUM_COEF * m_emb[:, 48000:48192] + MEAN * un[250:251, 0:192]
     stores[9].start()
 
-    each(sum_copy, G, "wait_recv")
+    for d in range(1, G):
+        sums_pass(d)
     for q in range(G):
         tot[q, 0:96, 0:96] = sums[q, 0:96, 0:96]
         tot[q, 96:144, 0:32] = sums[q, 0:48, 96:128]
@@ -321,11 +383,12 @@
         new_emb[:, s * ROWS : (s + 1) * ROWS] = gath[s]
     stores[4].start()
 
-    each(left_copy, G, "wait_send")
+    left_wait_send()
     each(right_copy, G, "wait_send")
-    each(half_copy, G, "wait_send")
+    for n in range(1, 8):
+        near_copy(n).wait_send()
     each(quarter_copy, G, "wait_send")
-    each(sum_copy, G, "wait_send")
+    sums_wait_send()
     each(anchor_copy, F, "wait_send")
     each(total_copy, F, "wait_send")
 
@@ -389,10 +452,10 @@
             buf(144, 128), buf(144, 128), buf(144, 128), buf(1, 120), buf(1, 48192),
             buf(1, 1920), buf(3, 144, 128), buf(8, 8, 768), buf(8, 3072),
             buf(4, 128, 128), buf(4, 128, 128), buf(128, 128), buf(4, 112, 128), buf(4, 144, 128),
-            buf(4, 64, ROWS), buf(4, 2, 32, 256), buf(4, 2, 32, 256),
+            buf(4, 64, ROWS), buf(4, 8, 8, 256), buf(8, 4, 8, 256),
             buf(256, 256), buf(256, 256), buf(4, 48, ROWS),
             buf(F, 8, 640), buf(F, 8, 640), buf(F, 8, 640), buf(F, 8, 640), buf(F, 48, ROWS),
-            sem(16), sem(10), sem(G), sem(G), sem(G), sem(G), sem(G), sem(G), sem(G), sem(G), sem(F), sem(F), sem(G), sem(G),
+            sem(16), sem(10), sem(G), sem(G), sem(G), sem(G), sem(G), sem(G), sem(G), sem(8), sem(8), sem(F), sem(F), sem(G), sem(G), sem(G),
             sem(F), sem(F), sem(4), sem(F), sem(F), sem(F),
         ],
         compiler_params=pltpu.CompilerParams(collective_id=0, has_side_effects=True, vmem_limit_bytes=60 * 2**20),

time: 68.8 us -> 71 us (1.032)
  the two profiles are of different devices: /device:TPU:317 before, /device:TPU:57 now
where the time goes in v3:
time: 71 us; the launch traced here: 70.8 us
  Pallas kernels  70.1 us (99%)
    pallas_call x1, Pallas kernels, on_device(): pl.pallas_call(kernel, out_shape=results, in_specs=[hbm] * 16, out_specs=...  67.7 us
    pallas_call x1, Pallas kernels, on_device(): pl.pallas_call(write_out, out_shape=results, in_specs=[hbm] * 10, out_spe...  2.49 us

profile of v3, /device:TPU:57, one launch (start us, length us, event | category | flops | bytes accessed | tf_op | source)
XLA Modules:
  0.0 70.8 jit_solution(3789367776736519875)
XLA Ops:
  0.6 67.7 %outer_step.1 = (f32[192,96]{1,0:T(8,128)}, f32[48,384]{1,0:T(8,128)}, f32[192,96]{1,0:T(8,128)}, f32[15,128]{1,0:T(8,128)}, f32[48,4016]{1,0:T(8,128)}, /*index...) custom-call(f32[192,96]{1,0:T(8,128)} %bitcast.28, ...), custom_call_target="tpu_custom_call" | custom-call | tf_op jit(solution)/shard_map/outer_step/pallas_call | solution.py:443
  68.3 2.5 %write_out.1 = (f32[192,96]{1,0:T(8,128)}, f32[48,384]{1,0:T(8,128)}, f32[192,96]{1,0:T(8,128)}, f32[15,128]{1,0:T(8,128)}, f32[48,4016]{1,0:T(8,128)}, /*index=...) custom-call(f32[192,96]{1,0:T(8,128)} %get-tuple-element.30.refs_0_, ...), custom_call_target="tpu_custom_call" | custom-call | tf_op jit(solution)/shard_map/write_out/pallas_call | solution.py:470

commit v4 on v2

--- a/solution.py
+++ b/solution.py
@@ -92,12 +92,58 @@
     def _(d):
         pl.semaphore_signal(bar, inc=1, device_id={"rep": peer_g(d)}, device_id_type=pl.DeviceIdType.MESH)
 
-    for load in loads[:6]:
+    for load in loads[:2]:
         load.wait()
     for q in range(G):
         for h in range(2):
             rts_own[q, h, :, 0:192] = right[h * 32 : (h + 1) * 32, q * 192 : (q + 1) * 192]
     rts[g] = rts_own[g]
+
+    pl.semaphore_wait(bar, F + G - 2)
+
+    def rep_copy(src, dst, ss, rs, d):
+        return pltpu.make_async_remote_copy(
+            src_ref=src, dst_ref=dst, send_sem=ss.at[d], recv_sem=rs.at[d],
+            device_id={"rep": peer_g(d)}, device_id_type=pl.DeviceIdType.MESH)
+
+    def left_copy(d):
+        return rep_copy(lts.at[g], lts.at[g], l_ss, l_rs, d)
+
+    def right_copy(d):
+        return rep_copy(rts_own.at[peer_g(d), c], rts.at[g, c], r_ss, r_rs, d)
+
+    def quarter_copy(d):
+        return rep_copy(quart.at[peer_g(d)], quart_in.at[g], q_ss, q_rs, d)
+
+    def sum_copy(d):
+        return rep_copy(own_sum.at[pl.ds(0, 112)], sums.at[g], s_ss, s_rs, d)
+
+    def half_copy(d):
+        part = rts.at[peer_g(G - d), c]
+        return pltpu.make_async_remote_copy(
+            src_ref=part, dst_ref=part, send_sem=x_ss.at[d], recv_sem=x_rs.at[d],
+            device_id={"fsdp": f + 1 - 2 * c}, device_id_type=pl.DeviceIdType.MESH)
+
+    def anchor_copy(d):
+        return pltpu.make_async_remote_copy(
+            src_ref=amsg.at[peer_f(d)], dst_ref=arecv.at[f], send_sem=a_ss.at[d], recv_sem=a_rs.at[d],
+            device_id={"fsdp": peer_f(d)}, device_id_type=pl.DeviceIdType.MESH)
+
+    def total_copy(d):
+        return pltpu.make_async_remote_copy(
+            src_ref=umsg.at[peer_f(d)], dst_ref=urecv.at[f], send_sem=u_ss.at[d], recv_sem=u_rs.at[d],
+            device_id={"fsdp": peer_f(d)}, device_id_type=pl.DeviceIdType.MESH)
+
+    def each(copy, n, what):
+        @pl.loop(1, n)
+        def _(d):
+            getattr(copy(d), what)()
+
+    each(right_copy, G, "start")
+    each(left_copy, G, "start")
+
+    for load in loads[2:6]:
+        load.wait()
 
     for t in range(F):
         quart[0, 112 + t : 113 + t, 0:120] = d_small[:, t * 120 : (t + 1) * 120]
@@ -115,48 +161,11 @@
             quart[q, 112:128, 0:120] = small
     quart_in[g] = quart[g]
 
-    pl.semaphore_wait(bar, F + G - 2)
-
-    def rep_copy(src, dst, ss, rs, d):
-        return pltpu.make_async_remote_copy(
-            src_ref=src, dst_ref=dst, send_sem=ss.at[d], recv_sem=rs.at[d],
-            device_id={"rep": peer_g(d)}, device_id_type=pl.DeviceIdType.MESH)
-
-    def left_copy(d):
-        return rep_copy(lts.at[g], lts.at[g], l_ss, l_rs, d)
-
-    def right_copy(d):
-        return rep_copy(rts_own.at[peer_g(d), c], rts.at[g, c], r_ss, r_rs, d)
-
-    def quarter_copy(d):
-        return rep_copy(quart.at[peer_g(d)], quart_in.at[g], q_ss, q_rs, d)
-
-    def sum_copy(d):
-        return rep_copy(own_sum.at[pl.ds(0, 112)], sums.at[g], s_ss, s_rs, d)
-
-    def half_copy(d):
-        part = rts.at[peer_g(G - d), c]
-        return pltpu.make_async_remote_copy(
-            src_ref=part, dst_ref=part, send_sem=x_ss.at[d], recv_sem=x_rs.at[d],
-            device_id={"fsdp": f + 1 - 2 * c}, device_id_type=pl.DeviceIdType.MESH)
-
-    def anchor_copy(d):
-        return pltpu.make_async_remote_copy(
-            src_ref=amsg.at[peer_f(d)], dst_ref=arecv.at[f], send_sem=a_ss.at[d], recv_sem=a_rs.at[d],
-            device_id={"fsdp": peer_f(d)}, device_id_type=pl.DeviceIdType.MESH)
-
-    def total_copy(d):
-        return pltpu.make_async_remote_copy(
-            src_ref=umsg.at[peer_f(d)], dst_ref=urecv.at[f], send_sem=u_ss.at[d], recv_sem=u_rs.at[d],
-            device_id={"fsdp": peer_f(d)}, device_id_type=pl.DeviceIdType.MESH)
-
-    def each(copy, n, what):
-        @pl.loop(1, n)
-        def _(d):
-            getattr(copy(d), what)()
-
-    each(right_copy, G, "start")
-    each(left_copy, G, "start")
+    @pl.loop(1, G)
+    def _(d):
+        right_copy(d).wait_recv()
+        half_copy(d).start()
+
     each(quarter_copy, G, "start")
 
     for load in loads[6:]:
@@ -170,11 +179,6 @@
         base[pl.ds(2 * p + 1, 1), 0:192] = x[:, 192:384]
 
     base[250:251, 0:192] = a_emb[:, 48000:48192] - KEEP * m_emb[:, 48000:48192]
-
-    @pl.loop(1, G)
-    def _(d):
-        right_copy(d).wait_recv()
-        half_copy(d).start()
 
     amsg[...] = jnp.zeros((F, 8, 640), jnp.float32)
     lin[0] = a_attn[...] - KEEP * m_attn[...]
@@ -225,14 +229,38 @@
     sums[g] = own_sum[0:112, :]
     each(sum_copy, G, "start")
 
-    @pl.loop(0, 125, unroll=5)
-    def _(p):
-        at = pl.ds(pl.multiple_of(p * 384, 128), 384)
-        x = jnp.concatenate([un[pl.ds(2 * p, 1), 0:192], un[pl.ds(2 * p + 1, 1), 0:192]], axis=1)
-        next_emb[:, at] = MOMENTUM_COEF * m_emb[:, at] + MEAN * x
-
-    next_emb[:, 48000:48192] = MOMENTUM_COEF * m_emb[:, 48000:48192] + MEAN * un[250:251, 0:192]
-    stores[9].start()
+    up = jnp.logical_and(g >= plane, g < G - 1)
+    down = jnp.logical_and(g <= plane, g > 0)
+
+    def up_copy(s):
+        return pltpu.make_async_remote_copy(
+            src_ref=gath.at[s], dst_ref=gath.at[s], send_sem=up_ss.at[s], recv_sem=e_rs.at[s],
+            device_id={"rep": jnp.minimum(g + 1, G - 1)}, device_id_type=pl.DeviceIdType.MESH)
+
+    def down_copy(s):
+        return pltpu.make_async_remote_copy(
+            src_ref=gath.at[s], dst_ref=gath.at[s], send_sem=dn_ss.at[s], recv_sem=e_rs.at[s],
+            device_id={"rep": jnp.maximum(g - 1, 0)}, device_id_type=pl.DeviceIdType.MESH)
+
+    def relay(lo, hi):
+        @pl.loop(lo, hi)
+        def _(k):
+            off = lax.div(k + 1, 2)
+            s = peer_f(jnp.where(lax.rem(k, 2) == 1, off, F - off))
+
+            @pl.when(jnp.logical_or(plane != g, s != f))
+            def _():
+                up_copy(s).wait_recv()
+
+            @pl.when(up)
+            def _():
+                up_copy(s).start()
+
+            @pl.when(down)
+            def _():
+                down_copy(s).start()
+
+    relay(0, 4)
 
     each(sum_copy, G, "wait_recv")
     for q in range(G):
@@ -247,37 +275,7 @@
     urecv[f] = umsg[f]
     each(total_copy, F, "start")
 
-    up = jnp.logical_and(g >= plane, g < G - 1)
-    down = jnp.logical_and(g <= plane, g > 0)
-
-    def up_copy(s):
-        return pltpu.make_async_remote_copy(
-            src_ref=gath.at[s], dst_ref=gath.at[s], send_sem=up_ss.at[s], recv_sem=e_rs.at[s],
-            device_id={"rep": jnp.minimum(g + 1, G - 1)}, device_id_type=pl.DeviceIdType.MESH)
-
-    def down_copy(s):
-        return pltpu.make_async_remote_copy(
-            src_ref=gath.at[s], dst_ref=gath.at[s], send_sem=dn_ss.at[s], recv_sem=e_rs.at[s],
-            device_id={"rep": jnp.maximum(g - 1, 0)}, device_id_type=pl.DeviceIdType.MESH)
-
-    def relay(lo, hi):
-        @pl.loop(lo, hi)
-        def _(k):
-            s = peer_f(k)
-
-            @pl.when(jnp.logical_or(plane != g, s != f))
-            def _():
-                up_copy(s).wait_recv()
-
-            @pl.when(up)
-            def _():
-                up_copy(s).start()
-
-            @pl.when(down)
-            def _():
-                down_copy(s).start()
-
-    relay(0, 6)
+    relay(4, 9)
 
     each(anchor_copy, F, "wait_recv")
     fixed = dot(arecv[...].reshape(128, 640)[:, 0:576], spread, 0, 0)
@@ -296,7 +294,16 @@
     for i in (0, 1, 2, 3, 8):
         stores[i].start()
 
-    relay(6, 11)
+    relay(9, 13)
+
+    @pl.loop(0, 125, unroll=5)
+    def _(p):
+        at = pl.ds(pl.multiple_of(p * 384, 128), 384)
+        x = jnp.concatenate([un[pl.ds(2 * p, 1), 0:192], un[pl.ds(2 * p + 1, 1), 0:192]], axis=1)
+        next_emb[:, at] = MOMENTUM_COEF * m_emb[:, at] + MEAN * x
+
+    next_emb[:, 48000:48192] = MOMENTUM_COEF * m_emb[:, 48000:48192] + MEAN * un[250:251, 0:192]
+    stores[9].start()
 
     each(total_copy, F, "wait_recv")
     for t in range(F):
@@ -316,7 +323,7 @@
     for i in (5, 6, 7):
         stores[i].start()
 
-    relay(11, F)
+    relay(13, F)
     for s in range(F):
         new_emb[:, s * ROWS : (s + 1) * ROWS] = gath[s]
     stores[4].start()

time: 68.8 us -> 70.4 us (1.023)
  the two profiles are of different devices: /device:TPU:317 before, /device:TPU:57 now
where the time goes in v4:
time: 70.4 us; the launch traced here: 69.2 us
  Pallas kernels  68.5 us (97%)
    pallas_call x1, Pallas kernels, on_device(): pl.pallas_call(kernel, out_shape=results, in_specs=[hbm] * 16, out_specs=...  66.1 us
    pallas_call x1, Pallas kernels, on_device(): pl.pallas_call(write_out, out_shape=results, in_specs=[hbm] * 10, out_spe...  2.49 us

profile of v4, /device:TPU:57, one launch (start us, length us, event | category | flops | bytes accessed | tf_op | source)
XLA Modules:
  0.0 69.2 jit_solution(1140091147030446935)
XLA Ops:
  0.6 66.1 %outer_step.1 = (f32[192,96]{1,0:T(8,128)}, f32[48,384]{1,0:T(8,128)}, f32[192,96]{1,0:T(8,128)}, f32[15,128]{1,0:T(8,128)}, f32[48,4016]{1,0:T(8,128)}, /*index...) custom-call(f32[192,96]{1,0:T(8,128)} %bitcast.28, ...), custom_call_target="tpu_custom_call" | custom-call | tf_op jit(solution)/shard_map/outer_step/pallas_call | solution.py:387
  66.7 2.5 %write_out.1 = (f32[192,96]{1,0:T(8,128)}, f32[48,384]{1,0:T(8,128)}, f32[192,96]{1,0:T(8,128)}, f32[15,128]{1,0:T(8,128)}, f32[48,4016]{1,0:T(8,128)}, /*index=...) custom-call(f32[192,96]{1,0:T(8,128)} %get-tuple-element.30.refs_0_, ...), custom_call_target="tpu_custom_call" | custom-call | tf_op jit(solution)/shard_map/write_out/pallas_call | solution.py:414

commit v5 on v4

--- a/solution.py
+++ b/solution.py
@@ -50,7 +50,7 @@
     m_attn, m_in, m_out, m_small, m_emb,
     flat_small, lin, wide, widef, quart, quart_in, own_sum, sums, tot, lts, rts_own, rts, base, un, et,
     amsg, arecv, umsg, urecv, gath,
-    in_s, out_s, q_ss, q_rs, l_ss, l_rs, r_ss, r_rs, x_ss, x_rs, a_ss, a_rs, s_ss, s_rs, u_ss, u_rs, e_ss, up_ss, dn_ss, e_rs,
+    in_s, out_s, q_ss, q_rs, lu_ss, ld_ss, l_rs, r_ss, r_rs, x_ss, x_rs, a_ss, a_rs, su_ss, sd_ss, s_rs, u_ss, u_rs, e_ss, up_ss, dn_ss, e_rs,
 ):
     f = lax.axis_index("fsdp")
     g = lax.axis_index("rep")
@@ -106,17 +106,63 @@
             src_ref=src, dst_ref=dst, send_sem=ss.at[d], recv_sem=rs.at[d],
             device_id={"rep": peer_g(d)}, device_id_type=pl.DeviceIdType.MESH)
 
-    def left_copy(d):
-        return rep_copy(lts.at[g], lts.at[g], l_ss, l_rs, d)
-
     def right_copy(d):
         return rep_copy(rts_own.at[peer_g(d), c], rts.at[g, c], r_ss, r_rs, d)
 
+    def line(blocks, up_ss, down_ss, rs):
+        def hop(k, step):
+            ss = up_ss if step > 0 else down_ss
+            return pltpu.make_async_remote_copy(
+                src_ref=blocks.at[k], dst_ref=blocks.at[k], send_sem=ss.at[k], recv_sem=rs.at[k],
+                device_id={"rep": jnp.clip(g + step, 0, G - 1)}, device_id_type=pl.DeviceIdType.MESH)
+
+        def own():
+            @pl.when(g < G - 1)
+            def _():
+                hop(g, 1).start()
+
+            @pl.when(g > 0)
+            def _():
+                hop(g, -1).start()
+
+        def pass_on(d):
+            low = jnp.maximum(g - d, 0)
+            high = jnp.minimum(g + d, G - 1)
+
+            @pl.when(g >= d)
+            def _():
+                hop(low, 1).wait_recv()
+
+                @pl.when(g < G - 1)
+                def _():
+                    hop(low, 1).start()
+
+            @pl.when(g + d < G)
+            def _():
+                hop(high, -1).wait_recv()
+
+                @pl.when(g > 0)
+                def _():
+                    hop(high, -1).start()
+
+        def wait_send():
+            @pl.loop(0, G)
+            def _(k):
+                @pl.when(jnp.logical_and(k <= g, g < G - 1))
+                def _():
+                    hop(k, 1).wait_send()
+
+                @pl.when(jnp.logical_and(k >= g, g > 0))
+                def _():
+                    hop(k, -1).wait_send()
+
+        return own, pass_on, wait_send
+
+    left_own, left_pass, left_wait_send = line(lts, lu_ss, ld_ss, l_rs)
+    sums_own, sums_pass, sums_wait_send = line(sums, su_ss, sd_ss, s_rs)
+
     def quarter_copy(d):
         return rep_copy(quart.at[peer_g(d)], quart_in.at[g], q_ss, q_rs, d)
-
-    def sum_copy(d):
-        return rep_copy(own_sum.at[pl.ds(0, 112)], sums.at[g], s_ss, s_rs, d)
 
     def half_copy(d):
         part = rts.at[peer_g(G - d), c]
@@ -140,7 +186,7 @@
             getattr(copy(d), what)()
 
     each(right_copy, G, "start")
-    each(left_copy, G, "start")
+    left_own()
 
     for load in loads[2:6]:
         load.wait()
@@ -166,6 +212,7 @@
         right_copy(d).wait_recv()
         half_copy(d).start()
 
+    left_pass(1)
     each(quarter_copy, G, "start")
 
     for load in loads[6:]:
@@ -179,6 +226,8 @@
         base[pl.ds(2 * p + 1, 1), 0:192] = x[:, 192:384]
 
     base[250:251, 0:192] = a_emb[:, 48000:48192] - KEEP * m_emb[:, 48000:48192]
+
+    left_pass(2)
 
     amsg[...] = jnp.zeros((F, 8, 640), jnp.float32)
     lin[0] = a_attn[...] - KEEP * m_attn[...]
@@ -200,7 +249,7 @@
     arecv[f] = amsg[f]
     each(anchor_copy, F, "start")
 
-    each(left_copy, G, "wait_recv")
+    left_pass(3)
     each(half_copy, G, "wait_recv")
     u_emb = dot(lts[...].reshape(256, ROWS), rts[...].reshape(256, 256)[:, 0:192], 0, 0)
     un[0:ROWS, 0:192] = u_emb
@@ -224,11 +273,6 @@
     def _():
         gath[f] = et[lax.rem(f, 4)]
 
-    each(quarter_copy, G, "wait_recv")
-    own_sum[...] = quart_in[0] + quart_in[1] + quart_in[2] + quart_in[3]
-    sums[g] = own_sum[0:112, :]
-    each(sum_copy, G, "start")
-
     up = jnp.logical_and(g >= plane, g < G - 1)
     down = jnp.logical_and(g <= plane, g > 0)
 
@@ -260,9 +304,28 @@
             def _():
                 down_copy(s).start()
 
-    relay(0, 4)
-
-    each(sum_copy, G, "wait_recv")
+    relay(0, 2)
+
+    each(quarter_copy, G, "wait_recv")
+    own_sum[...] = quart_in[0] + quart_in[1] + quart_in[2] + quart_in[3]
+    sums[g] = own_sum[0:112, :]
+    sums_own()
+
+    @pl.loop(0, 125, unroll=5)
+    def _(p):
+        at = pl.ds(pl.multiple_of(p * 384, 128), 384)
+        x = jnp.concatenate([un[pl.ds(2 * p, 1), 0:192], un[pl.ds(2 * p + 1, 1), 0:192]], axis=1)
+        next_emb[:, at] = MOMENTUM_COEF * m_emb[:, at] + MEAN * x
+
+    next_emb[:, 48000:48192] = MOMENTUM_COEF * m_emb[:, 48000:48192] + MEAN * un[250:251, 0:192]
+    stores[9].start()
+
+    relay(2, 6)
+    sums_pass(1)
+    relay(6, 8)
+    sums_pass(2)
+    relay(8, 10)
+    sums_pass(3)
     for q in range(G):
         tot[q, 0:96, 0:96] = sums[q, 0:96, 0:96]
         tot[q, 96:144, 0:32] = sums[q, 0:48, 96:128]
@@ -275,7 +338,7 @@
     urecv[f] = umsg[f]
     each(total_copy, F, "start")
 
-    relay(4, 9)
+    relay(10, 13)
 
     each(anchor_copy, F, "wait_recv")
     fixed = dot(arecv[...].reshape(128, 640)[:, 0:576], spread, 0, 0)
@@ -294,16 +357,7 @@
     for i in (0, 1, 2, 3, 8):
         stores[i].start()
 
-    relay(9, 13)
-
-    @pl.loop(0, 125, unroll=5)
-    def _(p):
-        at = pl.ds(pl.multiple_of(p * 384, 128), 384)
-        x = jnp.concatenate([un[pl.ds(2 * p, 1), 0:192], un[pl.ds(2 * p + 1, 1), 0:192]], axis=1)
-        next_emb[:, at] = MOMENTUM_COEF * m_emb[:, at] + MEAN * x
-
-    next_emb[:, 48000:48192] = MOMENTUM_COEF * m_emb[:, 48000:48192] + MEAN * un[250:251, 0:192]
-    stores[9].start()
+    relay(13, F)
 
     each(total_copy, F, "wait_recv")
     for t in range(F):
@@ -323,16 +377,15 @@
     for i in (5, 6, 7):
         stores[i].start()
 
-    relay(13, F)
     for s in range(F):
         new_emb[:, s * ROWS : (s + 1) * ROWS] = gath[s]
     stores[4].start()
 
-    each(left_copy, G, "wait_send")
+    left_wait_send()
     each(right_copy, G, "wait_send")
     each(half_copy, G, "wait_send")
     each(quarter_copy, G, "wait_send")
-    each(sum_copy, G, "wait_send")
+    sums_wait_send()
     each(anchor_copy, F, "wait_send")
     each(total_copy, F, "wait_send")
 
@@ -399,7 +452,7 @@
             buf(4, 64, ROWS), buf(4, 2, 32, 256), buf(4, 2, 32, 256),
             buf(256, 256), buf(256, 256), buf(4, 48, ROWS),
             buf(F, 8, 640), buf(F, 8, 640), buf(F, 8, 640), buf(F, 8, 640), buf(F, 48, ROWS),
-            sem(16), sem(10), sem(G), sem(G), sem(G), sem(G), sem(G), sem(G), sem(G), sem(G), sem(F), sem(F), sem(G), sem(G),
+            sem(16), sem(10), sem(G), sem(G), sem(G), sem(G), sem(G), sem(G), sem(G), sem(G), sem(G), sem(F), sem(F), sem(G), sem(G), sem(G),
             sem(F), sem(F), sem(4), sem(F), sem(F), sem(F),
         ],
         compiler_params=pltpu.CompilerParams(collective_id=0, has_side_effects=True, vmem_limit_bytes=60 * 2**20),

time: 70.4 us -> 75.5 us (1.072); the launches traced: 69.2 us -> 75.4 us
  Pallas kernels: 68.5 us -> 74.7 us
    pallas_call x1, Pallas kernels: 66.1 us -> 72.2 us  [on_device(): pl.pallas_call(kernel, out_shape=results, in_specs=[hbm] * 16, out_specs=...]
where the time goes in v5:
time: 75.5 us; the launch traced here: 75.4 us
  Pallas kernels  74.7 us (99%)
    pallas_call x1, Pallas kernels, on_device(): pl.pallas_call(kernel, out_shape=results, in_specs=[hbm] * 16, out_specs=...  72.2 us
    pallas_call x1, Pallas kernels, on_device(): pl.pallas_call(write_out, out_shape=results, in_specs=[hbm] * 10, out_spe...  2.49 us

profile of v5, /device:TPU:57, one launch (start us, length us, event | category | flops | bytes accessed | tf_op | source)
XLA Modules:
  0.0 75.4 jit_solution(5788987830324107940)
XLA Ops:
  0.6 72.2 %outer_step.1 = (f32[192,96]{1,0:T(8,128)}, f32[48,384]{1,0:T(8,128)}, f32[192,96]{1,0:T(8,128)}, f32[15,128]{1,0:T(8,128)}, f32[48,4016]{1,0:T(8,128)}, /*index...) custom-call(f32[192,96]{1,0:T(8,128)} %bitcast.28, ...), custom_call_target="tpu_custom_call" | custom-call | tf_op jit(solution)/shard_map/outer_step/pallas_call | solution.py:440
  72.9 2.5 %write_out.1 = (f32[192,96]{1,0:T(8,128)}, f32[48,384]{1,0:T(8,128)}, f32[192,96]{1,0:T(8,128)}, f32[15,128]{1,0:T(8,128)}, f32[48,4016]{1,0:T(8,128)}, /*index=...) custom-call(f32[192,96]{1,0:T(8,128)} %get-tuple-element.30.refs_0_, ...), custom_call_target="tpu_custom_call" | custom-call | tf_op jit(solution)/shard_map/write_out/pallas_call | solution.py:467

commit v6 on v2

--- a/solution.py
+++ b/solution.py
@@ -296,7 +296,7 @@
     for i in (0, 1, 2, 3, 8):
         stores[i].start()
 
-    relay(6, 11)
+    relay(6, F)
 
     each(total_copy, F, "wait_recv")
     for t in range(F):
@@ -316,7 +316,6 @@
     for i in (5, 6, 7):
         stores[i].start()
 
-    relay(11, F)
     for s in range(F):
         new_emb[:, s * ROWS : (s + 1) * ROWS] = gath[s]
     stores[4].start()

time: 68.8 us -> 69.1 us (level)
  no operation moved by 1% of the time
where the time goes in v6:
time: 69.1 us; the launch traced here: 69 us
  Pallas kernels  68.3 us (99%)
    pallas_call x1, Pallas kernels, on_device(): pl.pallas_call(kernel, out_shape=results, in_specs=[hbm] * 16, out_specs=...  65.8 us
    pallas_call x1, Pallas kernels, on_device(): pl.pallas_call(write_out, out_shape=results, in_specs=[hbm] * 10, out_spe...  2.49 us

profile of v6, /device:TPU:317, one launch (start us, length us, event | category | flops | bytes accessed | tf_op | source)
XLA Modules:
  0.0 69.0 jit_solution(10391011986906320749)
XLA Ops:
  0.6 65.8 %outer_step.1 = (f32[192,96]{1,0:T(8,128)}, f32[48,384]{1,0:T(8,128)}, f32[192,96]{1,0:T(8,128)}, f32[15,128]{1,0:T(8,128)}, f32[48,4016]{1,0:T(8,128)}, /*index...) custom-call(f32[192,96]{1,0:T(8,128)} %bitcast.28, ...), custom_call_target="tpu_custom_call" | custom-call | tf_op jit(solution)/shard_map/outer_step/pallas_call | solution.py:379
  66.5 2.5 %write_out.1 = (f32[192,96]{1,0:T(8,128)}, f32[48,384]{1,0:T(8,128)}, f32[192,96]{1,0:T(8,128)}, f32[15,128]{1,0:T(8,128)}, f32[48,4016]{1,0:T(8,128)}, /*index=...) custom-call(f32[192,96]{1,0:T(8,128)} %get-tuple-element.30.refs_0_, ...), custom_call_target="tpu_custom_call" | custom-call | tf_op jit(solution)/shard_map/write_out/pallas_call | solution.py:406
